TPU v7x, 32 devices: a whole 2x2x4 slice. The times are simulated.
32 devices in a mesh: dp: 2 (over y), fsdp: 16 (over z, x, core).
Axes of the slice: x: 2, y: 2, z: 4, core: 2. Of those that a mesh axis runs over, the one named last changes fastest.
Arguments:
- tokens: bfloat16 [64, 512, 768], P(('dp', 'fsdp')), may hold values from -6 to 6
- out_grad: bfloat16 [64, 512, 768], P(('dp', 'fsdp')), may hold values from -6 to 6
- lengths: int32 [64], P(('dp', 'fsdp')), may hold values from 128 to 512, as said below
- labels: int32 [64], P(('dp', 'fsdp')), may hold values from 0 to 2
- exit_layers: int32 [64], P(('dp', 'fsdp')), may hold values from 0 to 11, as said below
- mat_master: float32 [9984, 768], P('fsdp')
- mat_first: float32 [9984, 768], P('fsdp')
- mat_second: float32 [9984, 768], P('fsdp'), as said below
- vec_master: float32 [16, 768], P(None, 'fsdp')
- vec_first: float32 [16, 768], P(None, 'fsdp')
- vec_second: float32 [16, 768], P(None, 'fsdp'), as said below
- cls_bias: float32 [3], replicated, may hold values from -3 to 3
- cls_first: float32 [3], replicated
- cls_second: float32 [3], replicated, as said below
Outputs:
- block_out: bfloat16 [64, 512, 768], P(('dp', 'fsdp'))
- input_grad: bfloat16 [64, 512, 768], P(('dp', 'fsdp'))
- ramp_loss: float32 [], replicated
- mat_master_new: float32 [9984, 768], P('fsdp')
- mat_first_new: float32 [9984, 768], P('fsdp')
- mat_second_new: float32 [9984, 768], P('fsdp')
- mat_copy: bfloat16 [9984, 768], P('fsdp')
- vec_master_new: float32 [16, 768], P(None, 'fsdp')
- vec_first_new: float32 [16, 768], P(None, 'fsdp')
- vec_second_new: float32 [16, 768], P(None, 'fsdp')
- vec_copy: bfloat16 [16, 768], P(None, 'fsdp')
- cls_bias_new: float32 [3], replicated
- cls_first_new: float32 [3], replicated
- cls_second_new: float32 [3], replicated
Inputs may be any that keep to these rules, and one draw needn't show every extreme that they name: Keys at positions of lengths or later are padding; some sequence has 512 tokens and some 512 // 4. `exit_layers`: a sequence whose exit layer is below 6 has left the encoder and is out of the loss; some sequence exits at layer 0 and some at the last. `mat_second`: positive. `vec_second`: positive. `cls_second`: positive.
All inputs are finite; a program needn't handle non-finite values.
Results may differ from a plain program's by a relative error of at most 0.02.
Values may be sent and summed in bfloat16 or wider, within the bound.
No kernel may reach another device: no remote copies, remote signals or barrier semaphores. Data moves between devices by JAX's collectives and lax.ppermute only.
A program may use at most 192 MiB of HBM per device.

v0:
```python
import jax
import jax.numpy as jnp
from jax import lax
from jax.sharding import PartitionSpec as P

D = 768
H = 12
HD = 64
FF = 3072
LAYER = 6
NCLS = 3
L = 512
STEP = 10


BETA_ONE = 0.9
BETA_TWO = 0.999
ADAM_EPS = 1e-08
WEIGHT_DECAY = 0.01
LN_EPS = 1e-12
VEC_RATE = 0.5
MASK_FILL = -1000000000.0


def product(first_arg, second_arg):
    return jnp.dot(first_arg, second_arg, preferred_element_type=jnp.float32)


def product_last(first_arg, second_arg):
    return lax.dot_general(
        first_arg, second_arg, (((1,), (1,)), ((), ())), preferred_element_type=jnp.float32
    )


def product_first(first_arg, second_arg):
    return lax.dot_general(
        first_arg, second_arg, (((0,), (0,)), ((), ())), preferred_element_type=jnp.float32
    )


def norm_forward(hidden, gain_vec, shift_vec):
    centre = jnp.mean(hidden, axis=-1, keepdims=True)
    centred = hidden - centre
    spread = jnp.mean(centred * centred, axis=-1, keepdims=True)
    inv_dev = lax.rsqrt(spread + LN_EPS)
    normed = centred * inv_dev
    return (normed * gain_vec + shift_vec, normed, inv_dev)


def norm_backward(grad_in, normed, inv_dev, gain_vec):
    scaled = grad_in * gain_vec
    return inv_dev * (
        scaled
        - jnp.mean(scaled, axis=-1, keepdims=True)
        - normed * jnp.mean(scaled * normed, axis=-1, keepdims=True)
    )


def split_matrices(matrices):
    return (
        matrices[0:D],
        matrices[D : 2 * D],
        matrices[2 * D : 3 * D],
        matrices[3 * D : 4 * D],
        matrices[4 * D : 5 * D],
        matrices[5 * D : 5 * D + FF],
        matrices[5 * D + FF : 5 * D + 2 * FF],
    )


def split_vectors(vectors):
    inner_rows = FF // D
    values_f = vectors.astype(jnp.float32)
    return (
        values_f[0],
        values_f[1],
        values_f[2],
        values_f[3],
        values_f[4],
        values_f[5],
        values_f[6],
        values_f[7],
        values_f[8],
        values_f[9 : 9 + inner_rows].reshape(FF),
        vectors[9 + inner_rows : 9 + inner_rows + NCLS],
    )


def row_rates(row_index):
    base_rate = D ** (-0.5)
    return jnp.where(
        (row_index >= 3 * D) & (row_index < 4 * D),
        8.0 * base_rate,
        jnp.where(row_index >= 5 * D + FF, 1.5 * FF ** (-0.5), base_rate),
    )


def adam_update(master, first_mom, second_mom, grad_in, rate, decay):
    first_new = BETA_ONE * first_mom + (1.0 - BETA_ONE) * grad_in
    second_new = BETA_TWO * second_mom + (1.0 - BETA_TWO) * grad_in * grad_in
    fix_one = 1.0 - BETA_ONE**STEP
    fix_two = 1.0 - BETA_TWO**STEP
    direction = first_new / fix_one / (jnp.sqrt(second_new / fix_two) + ADAM_EPS)
    master_new = master - rate * (direction + decay * master)
    return (master_new, first_new, second_new)


def masked_scores(q_seq, k_seq, length):
    score_scale = HD ** (-0.5)
    scores = (
        jnp.einsum("qhd,khd->hqk", q_seq, k_seq, preferred_element_type=jnp.float32) * score_scale
    )
    key_valid = jnp.arange(q_seq.shape[0]) < length
    return jnp.where(key_valid[None, None, :], scores, MASK_FILL)


def attend(seq_parts):
    q_seq, k_seq, v_seq, length = seq_parts
    scores = masked_scores(q_seq, k_seq, length)
    row_max = jnp.max(scores, axis=-1, keepdims=True)
    exp_scores = jnp.exp(scores - row_max)
    exp_total = jnp.sum(exp_scores, axis=-1, keepdims=True)
    attn_probs = exp_scores / exp_total
    log_total = row_max + jnp.log(exp_total)
    context = jnp.einsum(
        "hqk,khd->qhd", attn_probs.astype(jnp.bfloat16), v_seq, preferred_element_type=jnp.float32
    )
    return (context.astype(jnp.bfloat16), log_total)


def attend_back(seq_parts):
    q_seq, k_seq, v_seq, length, log_total, grad_ctx = seq_parts
    score_scale = HD ** (-0.5)
    attn_probs = jnp.exp(masked_scores(q_seq, k_seq, length) - log_total)
    grad_probs = jnp.einsum("qhd,khd->hqk", grad_ctx, v_seq, preferred_element_type=jnp.float32)
    grad_values = jnp.einsum(
        "hqk,qhd->khd",
        attn_probs.astype(jnp.bfloat16),
        grad_ctx,
        preferred_element_type=jnp.float32,
    )
    grad_scores = attn_probs * (
        grad_probs - jnp.sum(attn_probs * grad_probs, axis=-1, keepdims=True)
    )
    rounded = grad_scores.astype(jnp.bfloat16)
    grad_query = (
        jnp.einsum("hqk,khd->qhd", rounded, k_seq, preferred_element_type=jnp.float32) * score_scale
    )
    grad_keys = (
        jnp.einsum("hqk,qhd->khd", rounded, q_seq, preferred_element_type=jnp.float32) * score_scale
    )
    return (
        grad_query.astype(jnp.bfloat16),
        grad_keys.astype(jnp.bfloat16),
        grad_values.astype(jnp.bfloat16),
    )


def on_device(
    tokens,
    out_grad,
    lengths,
    labels,
    exit_layers,
    mat_master,
    mat_first,
    mat_second,
    vec_master,
    vec_first,
    vec_second,
    cls_bias,
    cls_first,
    cls_second,
):
    seq_count = tokens.shape[0]
    tok_count = seq_count * L
    active = (exit_layers >= LAYER).astype(jnp.float32)
    mat_low = mat_master.astype(jnp.bfloat16)
    vec_low = vec_master.astype(jnp.bfloat16)
    matrices, vectors = (
        lax.all_gather(mat_low, "fsdp", axis=0, tiled=True),
        lax.all_gather(vec_low, "fsdp", axis=1, tiled=True),
    )
    w_query, w_key, w_value, w_out, w_pool, w_inner, w_outer = split_matrices(matrices)
    (
        b_query,
        b_value,
        b_out,
        gain_one,
        shift_one,
        b_outer,
        gain_two,
        shift_two,
        b_pool,
        b_inner,
        w_class,
    ) = split_vectors(vectors)
    token_rows = tokens.reshape(tok_count, D)
    query_rows = (product(token_rows, w_query) + b_query).astype(jnp.bfloat16)
    key_rows = product(token_rows, w_key).astype(jnp.bfloat16)
    value_rows = (product(token_rows, w_value) + b_value).astype(jnp.bfloat16)
    q_heads = query_rows.reshape(seq_count, L, H, HD)
    k_heads = key_rows.reshape(seq_count, L, H, HD)
    v_heads = value_rows.reshape(seq_count, L, H, HD)
    context, log_total = lax.map(attend, (q_heads, k_heads, v_heads, lengths))
    ctx_rows = context.reshape(tok_count, D)
    resid_attn = token_rows.astype(jnp.float32) + (product(ctx_rows, w_out) + b_out)
    normed_out, normed_one, inv_one = norm_forward(resid_attn, gain_one, shift_one)
    normed_low = normed_out.astype(jnp.bfloat16)
    inner_pre = product_last(normed_low, w_inner) + b_inner
    activated = jax.nn.gelu(inner_pre, approximate=False).astype(jnp.bfloat16)
    resid_ffn = normed_out + (product(activated, w_outer) + b_outer)
    layer_out, normed_two, inv_two = norm_forward(resid_ffn, gain_two, shift_two)
    block_out = layer_out.astype(jnp.bfloat16).reshape(seq_count, L, D)
    first_row = block_out[:, 0, :]
    pooled = jnp.tanh(product(first_row, w_pool) + b_pool)
    pooled_low = pooled.astype(jnp.bfloat16)
    logits = product_last(pooled_low, w_class) + cls_bias
    log_norm = jax.nn.logsumexp(logits, axis=-1)
    onehot = (labels[:, None] == jnp.arange(NCLS)[None, :]).astype(jnp.float32)
    cross_ent = log_norm - jnp.sum(logits * onehot, axis=-1)
    ce_sum = jnp.sum(active * cross_ent)
    class_error = active[:, None] * (jnp.exp(logits - log_norm[:, None]) - onehot)
    error_sum = jnp.sum(class_error, axis=0)
    ce_total, active_count, error_total = lax.psum(
        (ce_sum, jnp.sum(active), error_sum), ("dp", "fsdp")
    )
    matrices, vectors = (
        lax.all_gather(mat_low, "fsdp", axis=0, tiled=True),
        lax.all_gather(vec_low, "fsdp", axis=1, tiled=True),
    )
    w_query, w_key, w_value, w_out, w_pool, w_inner, w_outer = split_matrices(matrices)
    (
        b_query,
        b_value,
        b_out,
        gain_one,
        shift_one,
        b_outer,
        gain_two,
        shift_two,
        b_pool,
        b_inner,
        w_class,
    ) = split_vectors(vectors)
    grad_logit = (class_error / active_count).astype(jnp.bfloat16)
    grad_pool = product(grad_logit, w_class)
    grad_pre = (grad_pool * (1.0 - pooled * pooled)).astype(jnp.bfloat16)
    grad_b_pool = jnp.sum(grad_pre.astype(jnp.float32), axis=0)
    grad_w_pool = product_first(first_row, grad_pre)
    grad_w_class = product_first(grad_logit, pooled_low)
    grad_first = product_last(grad_pre, w_pool)
    grad_layer = out_grad.astype(jnp.float32).at[:, 0, :].add(grad_first).reshape(tok_count, D)
    grad_gain_two = jnp.sum(grad_layer * normed_two, axis=0)
    grad_shift_two = jnp.sum(grad_layer, axis=0)
    grad_resid_ffn = norm_backward(grad_layer, normed_two, inv_two, gain_two)
    grad_ffn = grad_resid_ffn.astype(jnp.bfloat16)
    grad_b_outer = jnp.sum(grad_ffn.astype(jnp.float32), axis=0)
    inner_again = product_last(normed_low, w_inner) + b_inner
    gelu_out, gelu_pull = jax.vjp(
        lambda inner_val: jax.nn.gelu(inner_val, approximate=False), inner_again
    )
    activ_again = gelu_out.astype(jnp.bfloat16)
    grad_w_outer = product_first(activ_again, grad_ffn)
    grad_activ = product_last(grad_ffn, w_outer)
    grad_inner = gelu_pull(grad_activ)[0].astype(jnp.bfloat16)
    grad_b_inner = jnp.sum(grad_inner.astype(jnp.float32), axis=0)
    grad_w_inner = product_first(grad_inner, normed_low)
    grad_normed = grad_resid_ffn + product(grad_inner, w_inner)
    grad_gain_one = jnp.sum(grad_normed * normed_one, axis=0)
    grad_shift_one = jnp.sum(grad_normed, axis=0)
    grad_resid_attn = norm_backward(grad_normed, normed_one, inv_one, gain_one)
    grad_attn = grad_resid_attn.astype(jnp.bfloat16)
    grad_b_out = jnp.sum(grad_attn.astype(jnp.float32), axis=0)
    grad_w_out = product_first(ctx_rows, grad_attn)
    grad_ctx = product_last(grad_attn, w_out).astype(jnp.bfloat16).reshape(seq_count, L, H, HD)
    grad_q, grad_k, grad_v = lax.map(
        attend_back, (q_heads, k_heads, v_heads, lengths, log_total, grad_ctx)
    )
    grad_q = grad_q.reshape(tok_count, D)
    grad_k = grad_k.reshape(tok_count, D)
    grad_v = grad_v.reshape(tok_count, D)
    grad_b_query = jnp.sum(grad_q.astype(jnp.float32), axis=0)
    grad_b_value = jnp.sum(grad_v.astype(jnp.float32), axis=0)
    grad_w_query = product_first(token_rows, grad_q)
    grad_w_key = product_first(token_rows, grad_k)
    grad_w_value = product_first(token_rows, grad_v)
    grad_tokens = (
        grad_resid_attn
        + product_last(grad_q, w_query)
        + product_last(grad_k, w_key)
        + product_last(grad_v, w_value)
    )
    input_grad = grad_tokens.astype(jnp.bfloat16).reshape(seq_count, L, D)
    mat_grad = jnp.concatenate(
        [
            grad_w_query,
            grad_w_key,
            grad_w_value,
            grad_w_out,
            grad_w_pool,
            grad_w_inner,
            grad_w_outer,
        ],
        axis=0,
    )
    head_rows = jnp.stack(
        [
            grad_b_query,
            grad_b_value,
            grad_b_out,
            grad_gain_one,
            grad_shift_one,
            grad_b_outer,
            grad_gain_two,
            grad_shift_two,
            grad_b_pool,
        ],
        axis=0,
    )
    vec_grad = jnp.concatenate([head_rows, grad_b_inner.reshape(FF // D, D), grad_w_class], axis=0)
    mat_part, vec_part = (
        lax.psum_scatter(
            mat_grad.astype(jnp.bfloat16), "fsdp", scatter_dimension=0, tiled=True
        ).astype(jnp.float32),
        lax.psum_scatter(
            vec_grad.astype(jnp.bfloat16), "fsdp", scatter_dimension=1, tiled=True
        ).astype(jnp.float32),
    )
    mat_total, vec_total = (
        lax.psum(mat_part.astype(jnp.bfloat16), "dp").astype(jnp.float32),
        lax.psum(vec_part.astype(jnp.bfloat16), "dp").astype(jnp.float32),
    )
    ramp_loss = ce_total / active_count
    cls_grad = error_total / active_count
    shard_rows = mat_master.shape[0]
    row_index = lax.axis_index("fsdp") * shard_rows + jnp.arange(shard_rows)
    rates = row_rates(row_index)[:, None]
    mat_new, mat_first_new, mat_second_new = adam_update(
        mat_master, mat_first, mat_second, mat_total, rates, WEIGHT_DECAY
    )
    vec_new, vec_first_new, vec_second_new = adam_update(
        vec_master, vec_first, vec_second, vec_total, VEC_RATE, 0.0
    )
    cls_new, cls_first_new, cls_second_new = adam_update(
        cls_bias, cls_first, cls_second, cls_grad, VEC_RATE, 0.0
    )
    return (
        block_out,
        input_grad,
        ramp_loss,
        mat_new,
        mat_first_new,
        mat_second_new,
        mat_new.astype(jnp.bfloat16),
        vec_new,
        vec_first_new,
        vec_second_new,
        vec_new.astype(jnp.bfloat16),
        cls_new,
        cls_first_new,
        cls_second_new,
    )


def solution(mesh):
    placed = (
        P(("dp", "fsdp"), None, None),
        P(("dp", "fsdp"), None, None),
        P(("dp", "fsdp")),
        P(("dp", "fsdp")),
        P(("dp", "fsdp")),
        P("fsdp", None),
        P("fsdp", None),
        P("fsdp", None),
        P(None, "fsdp"),
        P(None, "fsdp"),
        P(None, "fsdp"),
        P(),
        P(),
        P(),
    )
    return jax.shard_map(
        on_device,
        mesh=mesh,
        in_specs=placed,
        out_specs=(
            P(("dp", "fsdp"), None, None),
            P(("dp", "fsdp"), None, None),
            P(),
            P("fsdp", None),
            P("fsdp", None),
            P("fsdp", None),
            P("fsdp", None),
            P(None, "fsdp"),
            P(None, "fsdp"),
            P(None, "fsdp"),
            P(None, "fsdp"),
            P(),
            P(),
            P(),
        ),
        check_vma=False,
    )
```

profile of v0, /device:TPU:0, one launch (start us, length us, event | category | flops | bytes accessed | tf_op | source)
XLA Modules:
  0.0 690.1 jit_solution(1368104361643564995)
XLA Ops:
  10.0 23.6 %all-gather = bf16[16,48,16]{1,2,0:T(8,128)(2,1)S(1)} all-gather(bf16[1,48,16]{1,2,0:T(8,128)(2,1)S(1)} %convert_bitcast_fusion), channel_id=1, replica_groups=mesh['dp'=2,'fsdp'=16] {'fsdp'}, dimensions={0}, use_global_device_ids=true | all-gather | bytes 26112 | tf_op jit(solution)/shard_map/all_gather | solution.py:182
  38.3 93.3 %all-gather.3.cloned.1.call-done = bf16[9984,768]{1,0:T(8,128)(2,1)} async-done(((bf16[624,768]{1,0:T(8,128)(2,1)}), bf16[9984,768]{1,0:T(8,128)(2,1)}) %all-gather.3.cloned.1.call-update) | async-done | bytes 15335440 | tf_op jit(solution)/shard_map/all_gather | solution.py:181
  155.4 22.9 %while.27 = (s32[]{:T(128)}, bf16[2,512,12,64]{1,3,2,0:T(8,128)(2,1)}, f32[2,12,512,1]{2,1,3,0:T(8,128)S(1)}, bf16[2,512,12,64]{1,3,2,0:T(8,128)(2,1)}, s32[2]{0...) while((s32[]{:T(128)}, ...), condition=%wide.region_3.4_spmd, body=%wide.region_0.3_spmd.sunk | while | flops 843442688 | bytes 47427716 | solution.py:205
  187.1 36.7 %multiply_convert_fusion.3 = (bf16[1024,3072]{1,0:T(8,128)(2,1)S(1)}, f32[1024,3072]{1,0:T(8,128)}, f32[1024,3072]{1,0:T(8,128)}) fusion(f32[3072]{0:T(1024)S(1)} %add.241, bf16[9984,768]{1,0:T(8,128)(2,1)} %all-gather.3.cloned.1.call-done, f32[1024,768]{1,0:T(8,128)S(1)} %get-tuple-element.291, f32[768]{0:T(1024)S(1)} %get-tuple-element.220, ...), kind=kOutput, calls=%fused_computation.65 | convolution fusion | flops 5043388416 | bytes 39348224 | tf_op jit(solution)/shard_map/dot_general | solution.py:30
  223.9 9.9 %fusion.139 = (f32[1024]{0:T(1024)S(1)}, f32[1024,768]{1,0:T(8,128)S(1)}) fusion(f32[768]{0:T(1024)S(1)} %copy-done.61, bf16[1024,3072]{1,0:T(8,128)(2,1)S(1)} %get-tuple-element.284, bf16[9984,768]{1,0:T(8,128)(2,1)} %all-gather.3.cloned.1.call-done, f32[768]{0:T(1024)S(1)} %get-tuple-element.220, f32[768]{0:T(1024)S(1)} %get-tuple-element.221, ...), kind=kOutput, calls=%fused_computation.220 | convolution fusion | flops 4837342208 | bytes 17323008 | tf_op jit(solution)/shard_map/dot_general | solution.py:26
  239.0 39.1 %all-reduce = (f32[]{:T(128)}, f32[]{:T(128)}, f32[3]{0:T(128)}) all-reduce(f32[]{:T(128)} %get-tuple-element.228, f32[]{:T(128)} %get-tuple-element.227, f32[3]{0:T(128)S(1)} %get-tuple-element.281), channel_id=1, replica_groups=mesh['dp'=2,'fsdp'=16] {'dp','fsdp'}, use_global_device_ids=true, to_apply=%region_11.12 | all-reduce | flops 5 | bytes 40 | tf_op jit(solution)/shard_map/psum | solution.py:225
  289.1 4.3 convert_reduce_fusion.1
  293.4 19.4 %fusion.142 = (bf16[3072]{0:T(1024)(128)(2,1)}, bf16[1024,3072]{1,0:T(8,128)(2,1)}) fusion(f32[1024,3072]{1,0:T(8,128)} %get-tuple-element.285, bf16[9984,768]{1,0:T(8,128)(2,1)} %all-gather.3.cloned.1.call-done, f32[1024,768]{1,0:T(8,128)} %get-tuple-element.274, f32[1024,3072]{1,0:T(8,128)} %get-tuple-element.292, f32[3072]{0:T(1024)S(1)} %add.241), kind=kOutput, calls=%fused_computation.223 | convolution fusion | flops 4882953216 | bytes 39340032 | tf_op jit(solution)/shard_map/dot_general | solution.py:30
  312.8 10.5 %multiply_reduce_fusion.1 = (bf16[768]{0:T(1024)(128)(2,1)}, f32[1024]{0:T(1024)S(1)}, f32[1024]{0:T(1024)S(1)}, bf16[768]{0:T(1024)(128)(2,1)}, f32[1024,768]{1,0:T(8,128)S(1)}) fusion(f32[1024,768]{1,0:T(8,128)S(1)} %copy-done.14, f32[1024]{0:T(1024)S(1)} %add_rsqrt_fusion.1, f32[1024]{0:T(1024)S(1)} %broadcast_multiply_fusion.5, ...), kind=kOutput, calls=%fused_computation.93 | convolution fusion | flops 4839698432 | bytes 20469760 | tf_op jit(solution)/shard_map/dot_general | solution.py:26
  336.9 52.1 %while.28 = (s32[]{:T(128)}, bf16[2,512,12,64]{1,3,2,0:T(8,128)(2,1)}, bf16[2,512,12,64]{1,3,2,0:T(8,128)(2,1)}, bf16[2,512,12,64]{1,3,2,0:T(8,128)(2,1)}, bf16[...) while((s32[]{:T(128)}, ...), condition=%wide.region_18.19_spmd, body=%wide.region_16.18_spmd.sunk | while | flops 2062412288 | bytes 140180784 | solution.py:277
  340.0 7.3 %multiply_reduce_fusion.9 = (f32[12,512]{1,0:T(8,128)S(1)}, f32[12,512,512]{1,2,0:T(8,128)}) fusion(f32[12,512,512]{1,2,0:T(8,128)S(1)} %fusion.193, f32[12,512]{1,0:T(8,128)S(1)} %dynamic-slice_bitcast_fusion.2, pred[512]{0:T(512)(128)(4,1)S(1)} %iota_compare_fusion.6, bf16[2,512,12,64]{1,3,2,0:T(8,128)(2,1)S(1)} %copy-done.7, ...), kind=kOutput, calls=%fused_computation.23.clone.1 | convolution fusion | flops 418375680 | bytes 26797568 | tf_op jit(solution)/shard_map/while/body/eval_jaxpr/qhd,khd->hqk/dot_general | solution.py:135
  347.4 7.2 %multiply_convert_fusion.5 = bf16[12,512,512]{1,2,0:T(8,128)(2,1)S(1)} fusion(f32[12,512,512]{1,2,0:T(8,128)} %get-tuple-element.414, f32[12,512,512]{1,2,0:T(8,128)S(1)} %fusion.193, f32[12,512]{1,0:T(8,128)S(1)} %get-tuple-element.415, f32[12,512]{1,0:T(8,128)S(1)} %dynamic-slice_bitcast_fusion.2, pred[512]{0:T(512)(128)(4,1)S(1)} %iota_compare_fusion.6), kind=kLoop, calls=%fused_computation.22.clone.1 | loop fusion | flops 18874368 | bytes 31506944 | tf_op jit(solution)/shard_map/while/body/eval_jaxpr/convert_element_type | solution.py:145
  365.9 7.3 %multiply_reduce_fusion.9 = (f32[12,512]{1,0:T(8,128)S(1)}, f32[12,512,512]{1,2,0:T(8,128)}) fusion(f32[12,512,512]{1,2,0:T(8,128)S(1)} %fusion.193, f32[12,512]{1,0:T(8,128)S(1)} %dynamic-slice_bitcast_fusion.2, pred[512]{0:T(512)(128)(4,1)S(1)} %iota_compare_fusion.6, bf16[2,512,12,64]{1,3,2,0:T(8,128)(2,1)S(1)} %copy-done.7, ...), kind=kOutput, calls=%fused_computation.23.clone.1 | convolution fusion | flops 418375680 | bytes 26797568 | tf_op jit(solution)/shard_map/while/body/eval_jaxpr/qhd,khd->hqk/dot_general | solution.py:135
  373.2 7.2 %multiply_convert_fusion.5 = bf16[12,512,512]{1,2,0:T(8,128)(2,1)S(1)} fusion(f32[12,512,512]{1,2,0:T(8,128)} %get-tuple-element.414, f32[12,512,512]{1,2,0:T(8,128)S(1)} %fusion.193, f32[12,512]{1,0:T(8,128)S(1)} %get-tuple-element.415, f32[12,512]{1,0:T(8,128)S(1)} %dynamic-slice_bitcast_fusion.2, pred[512]{0:T(512)(128)(4,1)S(1)} %iota_compare_fusion.6), kind=kLoop, calls=%fused_computation.22.clone.1 | loop fusion | flops 18874368 | bytes 31506944 | tf_op jit(solution)/shard_map/while/body/eval_jaxpr/convert_element_type | solution.py:145
  408.5 7.8 %fusion.64 = bf16[9984,768]{1,0:T(8,128)(2,1)} fusion(bf16[9984,768]{1,0:T(8,128)(2,1)} %fusion.81, bf16[1024,3072]{1,0:T(8,128)(2,1)S(1)} %bitcast.232, f32[1024,768]{1,0:T(8,128)S(1)} %copy-done.15, f32[768]{0:T(1024)S(1)} %copy-done.60, f32[768]{0:T(1024)S(1)} %copy-done.43, f32[1024]{0:T(1024)S(1)} %copy-done.45, f32[1024]{0:T(1024)S(1)} %copy-done.37), kind=kOutput, calls=%fused_computation.82 | convolution fusion | flops 4838129664 | bytes 14170112 | tf_op jit(solution)/shard_map/dot_general | solution.py:36
  416.4 7.1 %fusion.63 = bf16[9984,768]{1,0:T(8,128)(2,1)} fusion(bf16[9984,768]{1,0:T(8,128)(2,1)} %fusion.64, bf16[1024,3072]{1,0:T(8,128)(2,1)S(1)} %bitcast.234, f32[1024,768]{1,0:T(8,128)S(1)} %copy-done.23), kind=kOutput, calls=%fused_computation.80 | convolution fusion | flops 4834983936 | bytes 14155776 | tf_op jit(solution)/shard_map/dot_general | solution.py:36
  427.7 5.0 fusion.100
  432.6 4.8 fusion.97
  437.4 141.5 %reduce-scatter.5.cloned.1.call-done = bf16[624,768]{1,0:T(8,128)(2,1)} async-done(((bf16[9984,768]{1,0:T(8,128)(2,1)}), bf16[624,768]{1,0:T(8,128)(2,1)}) %reduce-scatter.5.cloned.1.call-update) | async-done | bytes 958480 | tf_op jit(solution)/shard_map/reduce_scatter | solution.py:323
  581.6 6.3 add_convert_fusion.1
  588.0 47.8 %reduce-scatter.7.cloned.1.call-done = bf16[48,16]{1,0:T(8,128)(2,1)} async-done(((bf16[768,16]{1,0:T(8,128)(2,1)}), bf16[48,16]{1,0:T(8,128)(2,1)}) %reduce-scatter.7.cloned.1.call-update) | async-done | bytes 1552
  636.6 4.9 psum.38
  642.2 33.0 %all-reduce.3.cloned.1.call-done = bf16[624,768]{1,0:T(8,128)(2,1)} async-done(((bf16[624,768]{1,0:T(8,128)(2,1)}), bf16[624,768]{1,0:T(8,128)(2,1)}) %all-reduce.3.cloned.1.call-update) | async-done | bytes 958480 | tf_op jit(solution)/shard_map/psum | solution.py:331
  675.1 7.2 %fusion.133 = (bf16[624,768]{1,0:T(8,128)(2,1)}, f32[624,768]{1,0:T(8,128)}, f32[624,768]{1,0:T(8,128)}, f32[624,768]{1,0:T(8,128)}) fusion(f32[624,768]{1,0:T(8,128)} %param.25, f32[624]{0:T(1024)S(1)} %select_select_fusion, bf16[624,768]{1,0:T(8,128)(2,1)} %all-reduce.3.cloned.1.call-done, f32[624,768]{1,0:T(8,128)} %param.26, f32[624,768]{1,0:T(8,128)} %param.27), kind=kLoop, calls=%fused_computation.217 | loop fusion | flops 8146944 | bytes 13420992 | tf_op jit(solution)/shard_map/convert_element_type | solution.py:355
  (313 shorter events, 139.8 us)
Async XLA Ops:
  7.2 27.3 %copy-start.68 = (s32[2]{0:T(128)S(1)}, s32[2]{0:T(128)}, u32[]{:S(2)}) copy-start(s32[2]{0:T(128)} %param.24) | copy-start | bytes 28
  7.2 27.8 %copy-start.30 = (bf16[2,512,768]{2,1,0:T(8,128)(2,1)S(1)}, bf16[2,512,768]{2,1,0:T(8,128)(2,1)}, u32[]{:S(2)}) copy-start(bf16[2,512,768]{2,1,0:T(8,128)(2,1)} %param.21) | copy-start | bytes 4718596
  7.2 124.4 %all-gather.3.cloned.1.call-start = ((), (), s32[]{:S(2)}) async-start(), calls=%async_computation.2 | async-start | bytes 16293888 | tf_op jit(solution)/shard_map/all_gather | solution.py:181
  10.0 569.0 %reduce-scatter.5.cloned.1.call-start = ((), (), s32[]{:S(2)}) async-start(), calls=%async_computation.3 | async-start | bytes 16293888 | tf_op jit(solution)/shard_map/reduce_scatter | solution.py:323
  33.8 97.8 %copy-start.34 = (bf16[768,16]{0,1:T(8,128)(2,1)}, bf16[768,16]{0,1:T(8,128)(2,1)S(1)}, u32[]{:S(2)}) copy-start(bf16[768,16]{0,1:T(8,128)(2,1)S(1)} %reshape.228) | copy-start | bytes 73732
  34.5 189.3 %copy-start.59 = (f32[768]{0:T(1024)}, f32[768]{0:T(1024)S(1)}, u32[]{:S(2)}) copy-start(f32[768]{0:T(1024)S(1)} %get-tuple-element.220) | copy-start | bytes 9220
  34.5 288.7 %copy-start.42 = (f32[768]{0:T(1024)}, f32[768]{0:T(1024)S(1)}, u32[]{:S(2)}) copy-start(f32[768]{0:T(1024)S(1)} %get-tuple-element.221) | copy-start | bytes 9220
  186.5 37.3 %copy-start.13 = (f32[1024,768]{1,0:T(8,128)}, f32[1024,768]{1,0:T(8,128)S(1)}, u32[]{:S(2)}) copy-start(f32[1024,768]{1,0:T(8,128)S(1)} %get-tuple-element.291) | copy-start | bytes 9437188
  186.6 136.7 %copy-start.36 = (f32[1024]{0:T(1024)}, f32[1024]{0:T(1024)S(1)}, u32[]{:S(2)}) copy-start(f32[1024]{0:T(1024)S(1)} %broadcast_multiply_fusion.5) | copy-start | bytes 12292
  187.1 136.2 %copy-start.44 = (f32[1024]{0:T(1024)}, f32[1024]{0:T(1024)S(1)}, u32[]{:S(2)}) copy-start(f32[1024]{0:T(1024)S(1)} %add_rsqrt_fusion.1) | copy-start | bytes 12292
  187.1 36.8 %copy-start.61 = (f32[768]{0:T(1024)S(1)}, f32[768]{0:T(1024)}, u32[]{:S(2)}) copy-start(f32[768]{0:T(1024)} %get-tuple-element.219) | copy-start | bytes 9220
  236.2 47.9 %copy-start.40 = (bf16[2,1,768]{2,1,0:T(2,128)(2,1)}, bf16[2,1,768]{2,1,0:T(2,128)(2,1)S(1)}, u32[]{:S(2)}) copy-start(bf16[2,1,768]{2,1,0:T(2,128)(2,1)S(1)} %slice.126) | copy-start | bytes 9220
  237.8 46.4 %copy-start.56 = (f32[2,768]{1,0:T(2,128)}, f32[2,768]{1,0:T(2,128)S(1)}, u32[]{:S(2)}) copy-start(f32[2,768]{1,0:T(2,128)S(1)} %fusion.91) | copy-start | bytes 18436
  239.0 45.2 %copy-start.66 = (f32[2,3]{1,0:T(2,128)}, f32[2,3]{1,0:T(2,128)S(1)}, u32[]{:S(2)}) copy-start(f32[2,3]{1,0:T(2,128)S(1)} %get-tuple-element.282) | copy-start | bytes 76
  423.6 212.2 %reduce-scatter.7.cloned.1.call-start = ((), (), s32[]{:S(2)}) async-start(), calls=%async_computation.5 | async-start | bytes 208896
  427.6 247.5 %all-reduce.3.cloned.1.call-start = ((), (), s32[]{:S(2)}) async-start(), calls=%async_computation.4 | async-start | bytes 1916928 | tf_op jit(solution)/shard_map/psum | solution.py:331
  432.6 146.4 %copy-start.71 = (f32[3]{0:T(128)S(1)}, f32[3]{0:T(128)}, u32[]{:S(2)}) copy-start(f32[3]{0:T(128)} %param.31) | copy-start | bytes 40
  432.6 146.4 %copy-start.72 = (f32[3]{0:T(128)S(1)}, f32[3]{0:T(128)}, u32[]{:S(2)}) copy-start(f32[3]{0:T(128)} %param.32) | copy-start | bytes 40
  432.6 146.4 %copy-start.73 = (f32[3]{0:T(128)S(1)}, f32[3]{0:T(128)}, u32[]{:S(2)}) copy-start(f32[3]{0:T(128)} %param.33) | copy-start | bytes 40
  432.6 146.4 %copy-start.74 = (f32[3]{0:T(128)S(1)}, f32[3]{0:T(128)}, u32[]{:S(2)}) copy-start(f32[3]{0:T(128)} %get-tuple-element.265) | copy-start | bytes 40
  432.6 149.0 %copy-start.18 = (f32[1024,768]{1,0:T(8,128)S(1)}, f32[1024,768]{1,0:T(8,128)}, u32[]{:S(2)}) copy-start(f32[1024,768]{1,0:T(8,128)} %copy-done.16) | copy-start | bytes 9437188
  581.6 59.9 %copy-start.39 = (f32[16,48]{1,0:T(8,128)S(1)}, f32[16,48]{1,0:T(8,128)}, u32[]{:S(2)}) copy-start(f32[16,48]{1,0:T(8,128)} %param.28) | copy-start | bytes 9220
  581.6 59.9 %copy-start.54 = (f32[16,48]{1,0:T(8,128)S(1)}, f32[16,48]{1,0:T(8,128)}, u32[]{:S(2)}) copy-start(f32[16,48]{1,0:T(8,128)} %param.29) | copy-start | bytes 9220
  581.6 59.9 %copy-start.55 = (f32[16,48]{1,0:T(8,128)S(1)}, f32[16,48]{1,0:T(8,128)}, u32[]{:S(2)}) copy-start(f32[16,48]{1,0:T(8,128)} %param.30) | copy-start | bytes 9220
  (74 other events, 265.2 us)
Sparse Core Ops, SparseCore 0:
  10.9 120.6 all-gather.2
  423.6 155.3 reduce-scatter.4
  583.1 52.7 reduce-scatter.6
  638.0 37.0 all-reduce.2
where the time goes:
time: 698 us; the launch traced here: 690 us
  waiting for transfers between devices  316 us (45%)
  matrix products  188 us (27%)
  blocking collectives  67.7 us (10%)
  other arithmetic  51.2 us (7%)
  local copies, waits for them, and re-layouts  48.4 us (7%)
  between operations  17.7 us (3%)
    reduce_scatter x1, waiting for transfers between devices, on_device(): lax.psum_scatter(mat_grad.astype(jnp.bfloat16), 'fsdp', scatter_dimension...  142 us
    all_gather x1, waiting for transfers between devices, on_device(): lax.all_gather(mat_low, 'fsdp', axis=0, tiled=True)  93.3 us
    dot_general x8, matrix products, product_last(): lax.dot_general(first_arg, second_arg, (((1,), (1,)), ((), ())), preferre...  77.4 us
    unnamed x5, waiting for transfers between devices  47.9 us
    psum x1, blocking collectives, on_device(): lax.psum((ce_sum, jnp.sum(active), error_sum), ('dp', 'fsdp'))  39.1 us
    dot_general x8, matrix products, product(): return jnp.dot(first_arg, second_arg, preferred_element_type=jnp.float32)  36.4 us
    psum x1, waiting for transfers between devices, on_device(): lax.psum(mat_part.astype(jnp.bfloat16), 'dp').astype(jnp.float32)  33 us
    dot_general x8, matrix products, product_first(): lax.dot_general(first_arg, second_arg, (((0,), (0,)), ((), ())), preferre...  27.4 us
  transfers between devices with their start and end apart: 4, of which 4 were waited for; matrix products, arithmetic and copies ran while one was open for 4% of the time, Pallas kernels for 0%

commit v1 on v0

v1 whole, which is shorter than its diff:
```python
import functools
import math

import jax
import jax.numpy as jnp
from jax import lax
from jax.experimental import pallas as pl
from jax.experimental.pallas import tpu as pltpu
from jax.sharding import PartitionSpec as P

D, H, HD, FF, NCLS, L = 768, 12, 64, 3072, 3, 512
LAYER = 6
STEP = 10
BETA_ONE = 0.9
BETA_TWO = 0.999
ADAM_EPS = 1e-08
WEIGHT_DECAY = 0.01
VEC_RATE = 0.5
LN_EPS = 1e-12
MASK_FILL = -1e9
LOG2E = 1.4426950408889634
f32, bf16 = jnp.float32, jnp.bfloat16
NN = (((1,), (0,)), ((), ()))
NT = (((1,), (1,)), ((), ()))
TN = (((0,), (0,)), ((), ()))
def dot(a, b, dims=NN):
    return lax.dot_general(a, b, dims, preferred_element_type=f32)
ANY = pl.BlockSpec(memory_space=pl.ANY)
HBM = pl.BlockSpec(memory_space=pltpu.HBM)
MROWS = 5 * D + 2 * FF
SMEM = pl.BlockSpec(memory_space=pltpu.SMEM)
TILE = 256
R = 16
ERF_P = 0.3275911
ERF_A = (0.254829592, -0.284496736, 1.421413741, -1.453152027, 1.061405429)

class Loads:
    def __init__(self, plan, refs, place, dst, sems, low, high):
        self.items = []
        for j, (piece, src, count, row) in enumerate(plan.spans):
            if isinstance(row, int):
                first, last = max(row, low), min(row + count, high)
                if first >= last:
                    continue
                cond = None
                source = refs[piece].at[pl.ds(src + first - row, last - first)]
                target = dst.at[pl.ds(first - low, last - first)]
            else:
                shard, at = plan.locate(row, place)
                cond = (shard * plan.rows >= low) & (shard * plan.rows < high)
                source = refs[piece].at[pl.ds(plan.skip(src, row, place), count)]
                target = dst.at[pl.ds(pl.multiple_of(jnp.where(cond, at - low, 0), 16), count)]
            self.items.append((cond, pltpu.make_async_copy(source, target, sems.at[j])))

    def start(self):
        for cond, copy in self.items:
            if cond is None:
                copy.start()
            else:
                pl.when(cond)(copy.start)

    def wait(self):
        for cond, copy in self.items:
            if cond is None:
                copy.wait()
            else:
                pl.when(cond)(copy.wait)


class Plan:
    def __init__(self, spans, rows, first=0):
        self.spans, self.rows, self.first = spans, rows, first
        self.part_e = -(-(rows // 2 - first) // 16) * 16
        self.head_end = -(-3 * D // rows) * rows
        self.tail_start = 3 * D // rows * rows

    def locate(self, where, place):
        steps, other_x, other_core, part = where
        z, x, core, rep = (place[i] for i in range(4))
        flip = lambda bit, other: 1 - bit if other else bit
        shard = (lax.rem(z - steps + 4, 4) * 2 + flip(x, other_x)) * 2 + flip(core, other_core)
        low_e = 2 * self.first
        part_e, size_e = self.part_e, self.rows - low_e
        base = {
            "all": 0,
            "e": low_e,
            "c_mine": rep * self.first,
            "c_other": (1 - rep) * self.first,
            "e_mine": low_e + rep * (size_e - part_e),
            "e_other": low_e + (1 - rep) * part_e,
        }[part]
        return shard, shard * self.rows + base

    def skip(self, start, where, place):
        if where[3] != "e_other":
            return start
        return pl.multiple_of(start + (1 - place[3]) * (2 * (self.first + self.part_e) - self.rows), 16)


def attn_fwd_kernel(plan, n, place, lens, x_ref, vec_ref, *refs):
    pieces = refs[:n]; qkv_ref, ctx_ref, st_ref, w, sems = refs[n:]
    s = pl.program_id(0)
    @pl.when(s == 0)
    def _():
        ld = Loads(plan, pieces, place, w, sems, 0, plan.head_end)
        ld.start(); ld.wait()
    x = x_ref[0]
    for i, b in ((0, 0), (1, None), (2, 1)):
        r = dot(x, w[i * D:(i + 1) * D])
        if b is not None: r = r + vec_ref[b:b + 1]
        qkv_ref[0, :, i * D:(i + 1) * D] = r.astype(bf16)
    length = lens[s]
    lane = lax.broadcasted_iota(jnp.int32, (L, 128), 1)
    low = lane < HD
    valid = lax.broadcasted_iota(jnp.int32, (1, L), 1) < length
    ones = jnp.ones((L, 128), bf16)
    stats = jnp.zeros((L, 128), f32)
    scale = LOG2E * HD ** -0.5
    for p in range(H // 2):
        q2 = qkv_ref[0, :, p * 128:(p + 1) * 128]
        k2 = qkv_ref[0, :, D + p * 128:D + (p + 1) * 128]
        v2 = qkv_ref[0, :, 2 * D + p * 128:2 * D + (p + 1) * 128]
        va = jnp.concatenate([v2, ones], axis=1)
        outs = []
        for h in range(2):
            qm = jnp.where(low if h == 0 else ~low, q2, jnp.zeros_like(q2))
            sc = jnp.where(valid, dot(qm, k2, NT) * scale, MASK_FILL)
            top = jnp.max(sc, axis=1, keepdims=True)
            e = jnp.exp2(sc - top).astype(bf16)
            o = dot(e, va)
            tot = o[:, 128:]
            outs.append(o[:, :128] / tot)
            stats = jnp.where(lane == 2 * p + h, top + jnp.log2(tot), stats)
        ctx_ref[0, :, p * 128:(p + 1) * 128] = jnp.where(low, outs[0], outs[1]).astype(bf16)
    st_ref[0] = stats.T

def attn_fwd(plan, pieces, place, lengths, tokens, vec):
    n = len(pieces); S = tokens.shape[0]
    return pl.pallas_call(
        functools.partial(attn_fwd_kernel, plan, n), grid=(S,), name="attn_fwd",
        in_specs=[SMEM, SMEM, pl.BlockSpec((1, L, D), lambda s: (s, 0, 0)), pl.BlockSpec((16, D), lambda s: (0, 0))] + [HBM] * n,
        out_specs=[pl.BlockSpec((1, L, 3 * D), lambda s: (s, 0, 0)), pl.BlockSpec((1, L, D), lambda s: (s, 0, 0)), pl.BlockSpec((1, 128, L), lambda s: (s, 0, 0))],
        out_shape=[jax.ShapeDtypeStruct((S, L, 3 * D), bf16), jax.ShapeDtypeStruct((S, L, D), bf16), jax.ShapeDtypeStruct((S, 128, L), f32)],
        scratch_shapes=[pltpu.VMEM((plan.head_end, D), bf16), pltpu.SemaphoreType.DMA((len(plan.spans),))],
        compiler_params=pltpu.CompilerParams(vmem_limit_bytes=50 << 20),
        cost_estimate=pl.CostEstimate(flops=8 * 10 ** 9, bytes_accessed=14 * 10 ** 6, transcendentals=6 * 10 ** 6),
    )(place, lengths, tokens, vec, *pieces)

def norm(h):
    mu = jnp.mean(h, axis=1, keepdims=True)
    c = h - mu
    r = lax.rsqrt(jnp.mean(c * c, axis=1, keepdims=True) + LN_EPS)
    return c * r, r

def norm_back(g, xh, r, gain):
    a = g * gain
    return r * (a - jnp.mean(a, axis=1, keepdims=True) - xh * jnp.mean(a * xh, axis=1, keepdims=True))

def gelu_both(u):
    t = 1.0 / (1.0 + (ERF_P * 2 ** -0.5) * jnp.abs(u))
    bell = jnp.exp2(u * u * (-0.5 * LOG2E))
    a = [0.5 * v for v in ERF_A]
    poly = t * (a[0] + t * (a[1] + t * (a[2] + t * (a[3] + t * a[4]))))
    tail = poly * bell
    phi = jnp.where(u < 0, tail, 1.0 - tail)
    g = u * phi
    return g, phi + (u * bell) * (2 * math.pi) ** -0.5

def ffn_kernel(plan, n, tiles, low, place, labels, exits, count, cls, x_ref, c_ref, og_ref, vec_ref, *refs):
    pieces = refs[:n]
    out_ref, dh1_ref, dc_ref, vg_ref, sc_ref, gw_ref, w, sems, g_s, du_s, n1_s, df_s, da_s, cc_s, gp_s, dy_s, e_s, z_s, stage, osem = refs[n:]
    i = pl.program_id(0)
    ld = Loads(plan, pieces, place, w, sems, low, MROWS)
    @pl.when(i == 0)
    def _():
        ld.start()
        vg_ref[...] = jnp.zeros_like(vg_ref); sc_ref[...] = jnp.zeros_like(sc_ref)
        ld.wait()
    wo, wp, w1, w2 = 3 * D - low, 4 * D - low, 5 * D - low, 5 * D + FF - low
    vrow = lambda r: vec_ref[r:r + 1]
    rows = pl.ds(pl.multiple_of(i * TILE, TILE), TILE)
    c = c_ref[...]
    cc_s[rows] = c
    h1 = x_ref[...].astype(f32) + (dot(c, w[wo:wo + D]) + vrow(2))
    xh1, r1 = norm(h1)
    n1 = xh1 * vrow(3) + vrow(4)
    n1b = n1.astype(bf16)
    n1_s[rows] = n1b
    f = None
    for j in range(FF // D):
        u = dot(n1b, w[w1 + j * D:w1 + (j + 1) * D], NT) + vrow(9 + j)
        g, gp = gelu_both(u)
        gb = g.astype(bf16)
        g_s[rows, j * D:(j + 1) * D] = gb
        gp_s[:, j * D:(j + 1) * D] = gp
        part = dot(gb, w[w2 + j * D:w2 + (j + 1) * D])
        f = part if f is None else f + part
    xh2, r2 = norm(n1 + (f + vrow(5)))
    yb = (xh2 * vrow(6) + vrow(7)).astype(bf16)
    out_ref[...] = yb
    dy_s[...] = og_ref[...].astype(f32)
    per = L // TILE
    @pl.when(lax.rem(i, per) == 0)
    def _():
        s = i // per
        head = lax.broadcasted_iota(jnp.int32, (R, 1), 0) == 0
        act = jnp.where(head, jnp.where(exits[s] >= LAYER, 1.0, 0.0), 0.0)
        e8 = jnp.where(head, yb[:R].astype(f32), 0.0).astype(bf16)
        pool = jnp.tanh(dot(e8, w[wp:wp + D]) + vrow(8))
        pb = pool.astype(bf16).astype(f32)
        lg = [jnp.sum(pb * vrow(13 + k), axis=1, keepdims=True) + cls[k] for k in range(NCLS)]
        top = jnp.maximum(jnp.maximum(lg[0], lg[1]), lg[2])
        lse = top + jnp.log(jnp.exp(lg[0] - top) + jnp.exp(lg[1] - top) + jnp.exp(lg[2] - top))
        hot = [jnp.where(labels[s] == k, 1.0, 0.0) for k in range(NCLS)]
        ce = act * (lse - (lg[0] * hot[0] + lg[1] * hot[1] + lg[2] * hot[2]))
        err = [act * (jnp.exp(lg[k] - lse) - hot[k]) for k in range(NCLS)]
        lane = lax.broadcasted_iota(jnp.int32, (R, 128), 1)
        got = jnp.where(lane == 0, ce, 0.0)
        for k in range(NCLS): got = jnp.where(lane == 1 + k, err[k], got)
        sc_ref[...] += got
        dl = [(err[k] / count[0]).astype(bf16).astype(f32) for k in range(NCLS)]
        gpool = dl[0] * vrow(13) + dl[1] * vrow(14) + dl[2] * vrow(15)
        dz = (gpool * (1.0 - pool * pool)).astype(bf16)
        srow = pl.ds(pl.multiple_of(s * R, R), R)
        e_s[srow] = e8; z_s[srow] = dz
        vg_ref[8:9] += jnp.sum(dz.astype(f32), axis=0, keepdims=True)
        for k in range(NCLS): vg_ref[13 + k:14 + k] += jnp.sum(dl[k] * pb, axis=0, keepdims=True)
        dy_s[0:R] += dot(dz, w[wp:wp + D], NT)
    dy = dy_s[...]
    def vsum(r, v): vg_ref[r:r + 1] += jnp.sum(v, axis=0, keepdims=True)
    vsum(6, dy * xh2); vsum(7, dy)
    dh2 = norm_back(dy, xh2, r2, vrow(6))
    dfb = dh2.astype(bf16)
    df_s[rows] = dfb
    vsum(5, dfb.astype(f32))
    dn1 = dh2
    for j in range(FF // D):
        du = (dot(dfb, w[w2 + j * D:w2 + (j + 1) * D], NT) * gp_s[:, j * D:(j + 1) * D]).astype(bf16)
        du_s[rows, j * D:(j + 1) * D] = du
        vsum(9 + j, du.astype(f32))
        dn1 = dn1 + dot(du, w[w1 + j * D:w1 + (j + 1) * D])
    vsum(3, dn1 * xh1); vsum(4, dn1)
    dh1 = norm_back(dn1, xh1, r1, vrow(3))
    dh1_ref[...] = dh1
    dab = dh1.astype(bf16)
    da_s[rows] = dab
    vsum(2, dab.astype(f32))
    dc_ref[...] = dot(dab, w[wo:wo + D], NT).astype(bf16)
    @pl.when(i == tiles - 1)
    def _():
        C = 384
        def flush(slot, base):
            return pltpu.make_async_copy(stage.at[slot], gw_ref.at[pl.ds(base, C)], osem.at[slot])
        stage[0] = dot(e_s[:, 0:C], z_s[...], TN).astype(bf16); flush(0, 4 * D).start()
        stage[1] = dot(e_s[:, C:2 * C], z_s[...], TN).astype(bf16); flush(1, 4 * D + C).start()
        def grads(lhs, rhs, width, base):
            def step(r, _):
                slot = lax.rem(r, 2)
                at = pl.multiple_of(r * C, C)
                v = dot(lhs[:, pl.ds(at, C)], rhs[...], TN).astype(bf16)
                flush(slot, base).wait()
                stage[slot] = v
                flush(slot, pl.multiple_of(base + at, C)).start()
                return 0
            lax.fori_loop(0, width // C, step, 0)
        grads(cc_s, da_s, D, 3 * D)
        grads(du_s, n1_s, FF, 5 * D)
        grads(g_s, df_s, FF, 5 * D + FF)
        flush(0, 0).wait(); flush(1, 0).wait()

def ffn(plan, pieces, place, labels, exits, count, cls, x, ctx, og, vec, total):
    n = len(pieces); T = x.shape[0]; tiles = T // TILE; low = plan.tail_start
    tok = lambda dt: pl.BlockSpec((TILE, D), lambda i: (i, 0))
    return pl.pallas_call(
        functools.partial(ffn_kernel, plan, n, tiles, low), grid=(tiles,), name="ffn",
        in_specs=[SMEM] * 5 + [tok(0)] * 3 + [pl.BlockSpec((16, D), lambda i: (0, 0))] + [HBM] * n,
        out_specs=[tok(0), tok(0), tok(0), pl.BlockSpec((16, D), lambda i: (0, 0)), pl.BlockSpec((R, 128), lambda i: (0, 0)), ANY],
        out_shape=[jax.ShapeDtypeStruct((T, D), bf16), jax.ShapeDtypeStruct((T, D), f32), jax.ShapeDtypeStruct((T, D), bf16), jax.ShapeDtypeStruct((16, D), f32), jax.ShapeDtypeStruct((R, 128), f32), jax.ShapeDtypeStruct((total, D), bf16)],
        scratch_shapes=[pltpu.VMEM((MROWS - low, D), bf16), pltpu.SemaphoreType.DMA((len(plan.spans),)),
            pltpu.VMEM((T, FF), bf16), pltpu.VMEM((T, FF), bf16), pltpu.VMEM((T, D), bf16), pltpu.VMEM((T, D), bf16), pltpu.VMEM((T, D), bf16), pltpu.VMEM((T, D), bf16),
            pltpu.VMEM((TILE, FF), f32), pltpu.VMEM((TILE, D), f32), pltpu.VMEM((R * (T // L), D), bf16), pltpu.VMEM((R * (T // L), D), bf16),
            pltpu.VMEM((2, 384, D), bf16), pltpu.SemaphoreType.DMA((2,))],
        compiler_params=pltpu.CompilerParams(vmem_limit_bytes=60 << 20),
        cost_estimate=pl.CostEstimate(flops=33 * 10 ** 9, bytes_accessed=40 * 10 ** 6, transcendentals=6 * 10 ** 6),
    )(place, labels, exits, count, cls, x, ctx, og, vec, *pieces)

def attn_bwd_kernel(plan, n, S, place, lens, x_ref, qkv_ref, dc_ref, c_ref, st_ref, dh1_ref, *refs):
    pieces = refs[:n]; gw_in, dx_ref, vg_ref, gw_ref, w, sems, d_s, x_s, stage, osem = refs[n:]
    s = pl.program_id(0)
    ld = Loads(plan, pieces, place, w, sems, 0, plan.head_end)
    @pl.when(s == 0)
    def _():
        ld.start()
        vg_ref[...] = jnp.zeros_like(vg_ref)
    rows = pl.ds(pl.multiple_of(s * L, L), L)
    x_s[rows] = x_ref[0]
    length = lens[s]
    low = lax.broadcasted_iota(jnp.int32, (L, 128), 1) < HD
    valid = lax.broadcasted_iota(jnp.int32, (L, 1), 0) < length
    scale = LOG2E * HD ** -0.5
    for p in range(H // 2):
        sl = slice(p * 128, (p + 1) * 128)
        q2 = qkv_ref[0, :, sl]; k2 = qkv_ref[0, :, D + p * 128:D + (p + 1) * 128]; v2 = qkv_ref[0, :, 2 * D + p * 128:2 * D + (p + 1) * 128]
        dc2 = dc_ref[0, :, sl]
        prod = (dc2.astype(f32) * c_ref[0, :, sl].astype(f32)).T
        res = []
        for h in range(2):
            pick = low if h == 0 else ~low
            zero = jnp.zeros_like(q2)
            km = jnp.where(pick, k2, zero); vm = jnp.where(pick, v2, zero)
            delta = jnp.sum(prod[h * HD:(h + 1) * HD], axis=0, keepdims=True)
            st = jnp.where(valid, dot(km, q2, NT) * scale, MASK_FILL)
            pt = jnp.exp2(st - st_ref[0, 2 * p + h:2 * p + h + 1, :])
            dpt = dot(vm, dc2, NT)
            dst = (pt * (dpt - delta)).astype(bf16)
            res.append((dot(dst, k2, TN), dot(dst, q2), dot(pt.astype(bf16), dc2)))
        both = lambda t: jnp.where(low, res[0][t], res[1][t])
        d_s[rows, p * 128:(p + 1) * 128] = (both(0) * HD ** -0.5).astype(bf16)
        d_s[rows, D + p * 128:D + (p + 1) * 128] = (both(1) * HD ** -0.5).astype(bf16)
        d_s[rows, 2 * D + p * 128:2 * D + (p + 1) * 128] = both(2).astype(bf16)
    @pl.when(s == 0)
    def _(): ld.wait()
    dq, dk, dv = (d_s[rows, i * D:(i + 1) * D] for i in range(3))
    dx_ref[0] = (dh1_ref[0] + dot(dq, w[0:D], NT) + dot(dk, w[D:2 * D], NT) + dot(dv, w[2 * D:3 * D], NT)).astype(bf16)
    vg_ref[0:1] += jnp.sum(dq.astype(f32), axis=0, keepdims=True)
    vg_ref[1:2] += jnp.sum(dv.astype(f32), axis=0, keepdims=True)
    @pl.when(s == S - 1)
    def _():
        C = 384
        def flush(slot, base):
            return pltpu.make_async_copy(stage.at[slot], gw_ref.at[pl.ds(base, C)], osem.at[slot])
        for i in range(3):
            for r in range(2):
                v = dot(x_s[:, r * C:(r + 1) * C], d_s[:, i * D:(i + 1) * D], TN).astype(bf16)
                if i: flush(r, 0).wait()
                stage[r] = v
                flush(r, i * D + r * C).start()
        flush(0, 0).wait(); flush(1, 0).wait()

def attn_bwd(plan, pieces, place, lengths, tokens, qkv, dc, ctx, st, dh1, gw):
    n = len(pieces); S = tokens.shape[0]
    seq = lambda *sh: pl.BlockSpec((1,) + sh, lambda s: (s, 0, 0))
    return pl.pallas_call(
        functools.partial(attn_bwd_kernel, plan, n, S), grid=(S,), name="attn_bwd",
        in_specs=[SMEM, SMEM, seq(L, D), seq(L, 3 * D), seq(L, D), seq(L, D), seq(128, L), seq(L, D)] + [HBM] * n + [ANY],
        out_specs=[seq(L, D), pl.BlockSpec((8, D), lambda s: (0, 0)), ANY],
        out_shape=[jax.ShapeDtypeStruct((S, L, D), bf16), jax.ShapeDtypeStruct((8, D), f32), jax.ShapeDtypeStruct(gw.shape, bf16)],
        input_output_aliases={8 + n: 2},
        scratch_shapes=[pltpu.VMEM((plan.head_end, D), bf16), pltpu.SemaphoreType.DMA((len(plan.spans),)), pltpu.VMEM((S * L, 3 * D), bf16), pltpu.VMEM((S * L, D), bf16), pltpu.VMEM((2, 384, D), bf16), pltpu.SemaphoreType.DMA((2,))],
        compiler_params=pltpu.CompilerParams(vmem_limit_bytes=56 << 20),
        cost_estimate=pl.CostEstimate(flops=16 * 10 ** 9, bytes_accessed=24 * 10 ** 6, transcendentals=6 * 10 ** 6),
    )(place, lengths, tokens, qkv, dc, ctx, st, dh1, *pieces, gw)


FSDP = 16


def permute(axis, pairs, value, after):
    if after:
        value = lax.optimization_barrier((value, *after))[0]
    return lax.ppermute(value, axis, pairs)


def swap_core(value, *after):
    return permute("fsdp", [(i, i ^ 1) for i in range(FSDP)], value, after)


def swap_x(value, *after):
    return permute("fsdp", [(i, i ^ 2) for i in range(FSDP)], value, after)


def swap_y(value, *after):
    return permute("dp", [(0, 1), (1, 0)], value, after)


def next_z(value, *after):
    return permute("fsdp", [(i, (i + 4) % FSDP) for i in range(FSDP)], value, after)


def sum_small(value):
    value = value + swap_y(value)
    for bit in (1, 2, 4, 8):
        value = value + permute("fsdp", [(i, i ^ bit) for i in range(FSDP)], value, ())
    return value


def position():
    index = lax.axis_index("fsdp")
    return index // 4, index // 2 % 2, index % 2, lax.axis_index("dp")


def gather_pieces(shard, first):
    rows = shard.shape[0]
    plan = Plan([], rows, first)
    c, e, spans = first, plan.part_e, plan.spans
    size_e = rows - 2 * c
    rep = lax.axis_index("dp")
    low_e = shard[2 * c :]
    my_c = lax.dynamic_slice_in_dim(shard, rep * c, c)
    my_e = lax.dynamic_slice_in_dim(low_e, rep * (size_e - e), e)
    x0c, x0e = swap_x(my_c), swap_x(low_e)
    zc1, ze1 = next_z(my_c), next_z(my_e)
    ye1 = swap_y(ze1)
    xc1 = swap_x(zc1, x0c)
    zc2 = next_z(zc1, x0c)
    ze2 = next_z(ze1, x0e)
    y0 = swap_y(x0c)
    xe1 = swap_x(jnp.concatenate([ze1, ye1]), x0e)
    yc1 = swap_y(jnp.concatenate([zc1, xc1]))
    ye2 = swap_y(ze2, y0)
    xc2 = swap_x(zc2, xc1)
    zc3 = next_z(zc2, xc1)
    ze3 = next_z(ze2, xe1)
    xe2 = swap_x(jnp.concatenate([ze2, ye2]), xe1)
    ye3 = swap_y(ze3, yc1)
    yc2 = swap_y(jnp.concatenate([zc2, xc2]), yc1)
    xc3 = swap_x(zc3, xc2)
    xe3 = swap_x(jnp.concatenate([ze3, ye3]), xe2)
    yc3 = swap_y(jnp.concatenate([zc3, xc3]), yc2)
    pieces = []

    def both(value, *parts):
        for other_core, piece in ((0, value), (1, swap_core(value))):
            for start, count, steps, other_x, part in parts:
                spans.append((len(pieces), start, count, (steps, other_x, other_core, part)))
            pieces.append(piece)

    both(shard, (0, rows, 0, 0, "all"))
    both(x0c, (0, c, 0, 1, "c_mine"))
    both(x0e, (0, size_e, 0, 1, "e"))
    both(y0, (0, c, 0, 1, "c_other"))
    rounds = ((zc1, ze1, xc1, ye1, yc1, xe1), (zc2, ze2, xc2, ye2, yc2, xe2), (zc3, ze3, xc3, ye3, yc3, xe3))
    for k, (zc, ze, xc, ye, yc, xe) in enumerate(rounds, 1):
        both(zc, (0, c, k, 0, "c_mine"))
        both(ze, (0, e, k, 0, "e_mine"))
        both(xc, (0, c, k, 1, "c_mine"))
        both(ye, (0, size_e - e, k, 0, "e_other"))
        both(yc, (0, c, k, 0, "c_other"), (c, c, k, 1, "c_other"))
        both(xe, (0, e, k, 1, "e_mine"), (e, size_e - e, k, 1, "e_other"))
    return pieces, plan


def add_low(a, b):
    return (a.astype(f32) + b.astype(f32)).astype(bf16)


def scatter_sum(grads, rows, first):
    c, e = first, rows // 2 - first
    z, x, core, rep = position()
    stacked = grads.reshape(4, 2, 2, rows, D)
    cut = lax.dynamic_slice_in_dim
    ring_c = ring_e = None
    last = {"x": [], "y": [], "z": []}

    def link(name, swap, value):
        done = last[name]
        got = swap(value, *done[-2:-1])
        done.append(got)
        return got

    for k in (1, 2, 3, 0):
        target = lax.rem(z - k + 4, 4)

        def pick(at_x, at_core):
            return lax.dynamic_slice(stacked, (target, at_x, at_core, 0, 0), (1, 1, 1, rows, D)).reshape(rows, D)

        got = swap_core(jnp.concatenate([pick(x, 1 - core), pick(1 - x, 1 - core)]))
        own, other = add_low(got[:rows], pick(x, core)), add_low(got[rows:], pick(1 - x, core))
        yc = link("y", swap_y, jnp.concatenate([cut(own, (1 - rep) * c, c), cut(other, (1 - rep) * c, c)]))
        xe = link("x", swap_x, other[2 * c :])
        own_c, other_c = add_low(cut(own, rep * c, c), yc[:c]), add_low(cut(other, rep * c, c), yc[c:])
        own_e = add_low(own[2 * c :], xe)
        xc = link("x", swap_x, other_c)
        ye = link("y", swap_y, cut(own_e, (1 - rep) * e, e))
        sum_c = own_c.astype(f32) + xc.astype(f32)
        sum_e = cut(own_e, rep * e, e).astype(f32) + ye.astype(f32)
        if ring_c is not None:
            sum_c, sum_e = sum_c + ring_c.astype(f32), sum_e + ring_e.astype(f32)
        sum_c, sum_e = sum_c.astype(bf16), sum_e.astype(bf16)
        if k:
            ring_c, ring_e = link("z", next_z, sum_c), link("z", next_z, sum_e)
    back = swap_y(jnp.concatenate([sum_c, sum_e]))
    order = lambda a, b: [jnp.where(rep == 0, a, b), jnp.where(rep == 0, b, a)]
    return jnp.concatenate(order(sum_c, back[:c]) + order(sum_e, back[c:]))


def row_rates(row_index):
    base_rate = D ** (-0.5)
    return jnp.where(
        (row_index >= 3 * D) & (row_index < 4 * D),
        8.0 * base_rate,
        jnp.where(row_index >= 5 * D + FF, 1.5 * FF ** (-0.5), base_rate),
    )


def adam_update(master, first_mom, second_mom, grad_in, rate, decay):
    first_new = BETA_ONE * first_mom + (1.0 - BETA_ONE) * grad_in
    second_new = BETA_TWO * second_mom + (1.0 - BETA_TWO) * grad_in * grad_in
    fix_one = 1.0 - BETA_ONE**STEP
    fix_two = 1.0 - BETA_TWO**STEP
    direction = first_new / fix_one / (jnp.sqrt(second_new / fix_two) + ADAM_EPS)
    master_new = master - rate * (direction + decay * master)
    return (master_new, first_new, second_new)


def on_device(
    paths,
    tokens,
    out_grad,
    lengths,
    labels,
    exit_layers,
    mat_master,
    mat_first,
    mat_second,
    vec_master,
    vec_first,
    vec_second,
    cls_bias,
    cls_first,
    cls_second,
):
    seqs, toks = tokens.shape[0], tokens.shape[0] * L
    shard_rows, lanes = mat_master.shape[0], vec_master.shape[1]
    index = lax.axis_index("fsdp")
    place = jnp.stack(position()).astype(jnp.int32)
    active = jnp.sum((exit_layers >= LAYER).astype(f32))
    mat_low, vec_low = mat_master.astype(bf16), vec_master.astype(bf16)
    if paths:
        placed = lax.dynamic_update_slice(jnp.zeros((16, D), bf16), vec_low, (0, lanes * index))
        placed = jnp.where(lax.axis_index("dp") == 0, placed, jnp.zeros_like(placed))
        small = sum_small(jnp.concatenate([placed, jnp.full((8, D), active).astype(bf16)]))
        vectors, active_count = small[:16].astype(f32), small[16, 0].astype(f32)
        pieces, plan = gather_pieces(mat_low, paths[0])
    else:
        pieces = [lax.all_gather(mat_low, "fsdp", axis=0, tiled=True)]
        plan = Plan([(0, 0, MROWS, 0)], 3 * D)
        vectors = lax.all_gather(vec_low, "fsdp", axis=1, tiled=True).astype(f32)
        active_count = lax.psum(active, ("dp", "fsdp"))
    qkv, context, stats = attn_fwd(plan, pieces, place, lengths, tokens, vectors)
    block_out, grad_attn, grad_ctx, vec_grad, sums, mat_grad = ffn(
        plan,
        pieces,
        place,
        labels,
        exit_layers,
        active_count.reshape(1),
        cls_bias,
        tokens.reshape(toks, D),
        context.reshape(toks, D),
        out_grad.reshape(toks, D),
        vectors,
        MROWS,
    )
    input_grad, head_grad, mat_grad = attn_bwd(
        plan,
        pieces,
        place,
        lengths,
        tokens,
        qkv,
        grad_ctx.reshape(seqs, L, D),
        context,
        stats,
        grad_attn.reshape(seqs, L, D),
        mat_grad,
    )
    vec_grad = jnp.concatenate([head_grad[:2], vec_grad[2:]])
    sums = jnp.sum(sums, axis=0)
    if paths:
        mat_total = scatter_sum(mat_grad, shard_rows, paths[1]).astype(f32)
        small = sum_small(jnp.concatenate([vec_grad, jnp.pad(sums[None], ((0, 7), (0, D - 128)))]))
        vec_total = lax.dynamic_slice(small, (0, lanes * index), (16, lanes))
        sums = small[16, :4]
    else:
        part = lax.psum_scatter(mat_grad, "fsdp", scatter_dimension=0, tiled=True)
        mat_total = lax.psum(part, "dp").astype(f32)
        part = lax.psum_scatter(vec_grad.astype(bf16), "fsdp", scatter_dimension=1, tiled=True)
        vec_total = lax.psum(part, "dp").astype(f32)
        sums = lax.psum(sums[:4], ("dp", "fsdp"))
    ramp_loss = sums[0] / active_count
    cls_grad = sums[1:4] / active_count
    rates = row_rates(index * shard_rows + jnp.arange(shard_rows))[:, None]
    mat_new, mat_first_new, mat_second_new = adam_update(
        mat_master, mat_first, mat_second, mat_total, rates, WEIGHT_DECAY
    )
    vec_new, vec_first_new, vec_second_new = adam_update(
        vec_master, vec_first, vec_second, vec_total, VEC_RATE, 0.0
    )
    cls_new, cls_first_new, cls_second_new = adam_update(
        cls_bias, cls_first, cls_second, cls_grad, VEC_RATE, 0.0
    )
    return (
        block_out.reshape(seqs, L, D),
        input_grad,
        ramp_loss,
        mat_new,
        mat_first_new,
        mat_second_new,
        mat_new.astype(bf16),
        vec_new,
        vec_first_new,
        vec_second_new,
        vec_new.astype(bf16),
        cls_new,
        cls_first_new,
        cls_second_new,
    )


def solution(mesh):
    rows = P(("dp", "fsdp"), None, None)
    each = P(("dp", "fsdp"))
    mat, vec = P("fsdp", None), P(None, "fsdp")
    paths = (160, 160) if (mesh.shape["dp"], mesh.shape["fsdp"]) == (2, FSDP) else None
    return jax.shard_map(
        functools.partial(on_device, paths),
        mesh=mesh,
        in_specs=(rows, rows, each, each, each, mat, mat, mat, vec, vec, vec, P(), P(), P()),
        out_specs=(rows, rows, P(), mat, mat, mat, mat, vec, vec, vec, vec, P(), P(), P()),
        check_vma=False,
    )
```

time: 698 us -> 355 us (0.51)
  waiting for transfers between devices: 316 us -> 124 us
  matrix products: 188 us -> 0 us
  Pallas kernels: 0 us -> 120 us
  blocking collectives: 67.7 us -> 0 us
  starting transfers between devices: 0.16 us -> 67 us
  local copies, waits for them, and re-layouts: 48.4 us -> 9.55 us
  other arithmetic: 51.2 us -> 26.7 us
  between operations: 17.7 us -> 4.39 us
    dot_general x38 -> x0, matrix products: 188 us -> none  [the longest x8 77.4 us: product_last(): lax.dot_general(first_arg, second_arg, (((1,), (1,)), ((), ())), preferre...]
    reduce_scatter x1 -> x0, waiting for transfers between devices: 142 us -> none  [on_device(): lax.psum_scatter(mat_grad.astype(jnp.bfloat16), 'fsdp', scatter_dimension...]
    ppermute x0 -> x80, waiting for transfers between devices: none -> 124 us  [permute(): return lax.ppermute(value, axis, pairs)]
    pallas_call x0 -> x3, Pallas kernels: none -> 120 us  [the longest x1 64.4 us: ffn(): pl.pallas_call(functools.partial(ffn_kernel, plan, n, tiles, low), grid=(...]
    all_gather x1 -> x0, waiting for transfers between devices: 93.3 us -> none  [on_device(): lax.all_gather(mat_low, 'fsdp', axis=0, tiled=True)]
    ppermute x0 -> x80, starting transfers between devices: none -> 67 us  [permute(): return lax.ppermute(value, axis, pairs)]
    unnamed x5 -> x0, waiting for transfers between devices: 47.9 us -> none
    psum x2 -> x0, blocking collectives: 44.1 us -> none  [the longest x1 39.1 us: on_device(): lax.psum((ce_sum, jnp.sum(active), error_sum), ('dp', 'fsdp'))]
  transfers between devices with their start and end apart: 4 -> 80, of which waited for: 4 -> 36; matrix products, arithmetic and copies ran while one was open for 4% -> 6% of each run, Pallas kernels for 0% -> 0%
where the time goes in v1:
time: 355 us; the launch traced here: 352 us
  waiting for transfers between devices  124 us (35%)
  Pallas kernels  120 us (34%)
  starting transfers between devices  67 us (19%)
  other arithmetic  26.7 us (8%)
  local copies, waits for them, and re-layouts  9.55 us (3%)
  between operations  4.39 us (1%)
    ppermute x80, waiting for transfers between devices, permute(): return lax.ppermute(value, axis, pairs)  124 us
    ppermute x80, starting transfers between devices, permute(): return lax.ppermute(value, axis, pairs)  67 us
    pallas_call x1, Pallas kernels, ffn(): pl.pallas_call(functools.partial(ffn_kernel, plan, n, tiles, low), grid=(...  64.4 us
    pallas_call x1, Pallas kernels, attn_bwd(): pl.pallas_call(functools.partial(attn_bwd_kernel, plan, n, S), grid=(S,),...  38.4 us
    pallas_call x1, Pallas kernels, attn_fwd(): pl.pallas_call(functools.partial(attn_fwd_kernel, plan, n), grid=(S,), na...  17.4 us
    convert_element_type x9, other arithmetic, add_low(): return (a.astype(f32) + b.astype(f32)).astype(bf16)  7.3 us
  transfers between devices with their start and end apart: 80, of which 36 were waited for; matrix products, arithmetic and copies ran while one was open for 6% of the time, Pallas kernels for 0%

profile of v1, /device:TPU:0, one launch (start us, length us, event | category | flops | bytes accessed | tf_op | source)
XLA Modules:
  0.0 351.5 jit_solution(16801631620778996311)
XLA Ops:
  2.4 3.1 collective-permute-start.12
  16.7 7.0 %collective-permute-done.2 = bf16[24,768]{1,0:T(8,128)(2,1)S(1)} collective-permute-done((bf16[24,768]{1,0:T(8,128)(2,1)S(1)}, bf16[24,768]{1,0:T(8,128)(2,1)S(1)}, u32[]{:S(2)}, u32[]{:S(2)}) %collective-permute-start.2) | collective-permute-done | bytes 36896 | tf_op jit(solution)/shard_map/ppermute | solution.py:361
  36.6 3.3 collective-permute-done.24.refs_20_
  45.0 5.6 %collective-permute-done.26.refs_22_ = bf16[160,768]{1,0:T(8,128)(2,1)S(1)} collective-permute-done((bf16[160,768]{1,0:T(8,128)(2,1)S(1)}, bf16[160,768]{1,0:T(8,128)(2,1)S(1)}, u32[]{:S(2)}, u32[]{:S(2)}) %collective-permute-start.26) | collective-permute-done | bytes 245792 | tf_op jit(solution)/shard_map/ppermute | solution.py:361
  52.1 3.3 collective-permute-done.36.refs_32_
  59.0 9.1 %collective-permute-done.30.refs_26_ = bf16[160,768]{1,0:T(8,128)(2,1)S(1)} collective-permute-done((bf16[160,768]{1,0:T(8,128)(2,1)S(1)}, bf16[160,768]{1,0:T(8,128)(2,1)S(1)}, u32[]{:S(2)}, u32[]{:S(2)}) %collective-permute-start.30) | collective-permute-done | bytes 245792 | tf_op jit(solution)/shard_map/ppermute | solution.py:361
  69.1 7.2 %collective-permute-done.38.refs_34_ = bf16[160,768]{1,0:T(8,128)(2,1)S(1)} collective-permute-done((bf16[160,768]{1,0:T(8,128)(2,1)S(1)}, bf16[160,768]{1,0:T(8,128)(2,1)S(1)}, u32[]{:S(2)}, u32[]{:S(2)}) %collective-permute-start.38) | collective-permute-done | bytes 245792 | tf_op jit(solution)/shard_map/ppermute | solution.py:361
  78.9 8.5 %collective-permute-done.40.refs_36_ = bf16[160,768]{1,0:T(8,128)(2,1)S(1)} collective-permute-done((bf16[160,768]{1,0:T(8,128)(2,1)S(1)}, bf16[160,768]{1,0:T(8,128)(2,1)S(1)}, u32[]{:S(2)}, u32[]{:S(2)}) %collective-permute-start.40) | collective-permute-done | bytes 245792 | tf_op jit(solution)/shard_map/ppermute | solution.py:361
  87.4 4.5 %collective-permute-done.42.refs_38_ = bf16[160,768]{1,0:T(8,128)(2,1)S(1)} collective-permute-done((bf16[160,768]{1,0:T(8,128)(2,1)S(1)}, bf16[160,768]{1,0:T(8,128)(2,1)S(1)}, u32[]{:S(2)}, u32[]{:S(2)}) %collective-permute-start.42) | collective-permute-done | bytes 245792 | tf_op jit(solution)/shard_map/ppermute | solution.py:361
  98.9 8.7 %collective-permute-done.46.refs_42_ = bf16[320,768]{1,0:T(8,128)(2,1)} collective-permute-done((bf16[320,768]{1,0:T(8,128)(2,1)S(1)}, bf16[320,768]{1,0:T(8,128)(2,1)}, u32[]{:S(2)}, u32[]{:S(2)}) %collective-permute-start.46) | collective-permute-done | bytes 491552 | tf_op jit(solution)/shard_map/ppermute | solution.py:361
  112.9 17.4 %attn_fwd.1 = (bf16[2,512,2304]{2,1,0:T(8,128)(2,1)}, bf16[2,512,768]{2,1,0:T(8,128)(2,1)}, f32[2,128,512]{2,1,0:T(8,128)}) custom-call(s32[4]{0:T(128)S(1)} %pad_add_fusion.1.place, s32[2]{0:T(128)S(1)} %copy-done.20, bf16[2,512,768]{2,1,0:T(8,128)(2,1)} %x_ref.3, f32[16,768]{1,0:T(8,128)S(1)} %slice_convert_fusion.vec_ref, bf16[624,768]{1,0:T(8,128)(2,1)} %copy-done.22, ...), custom_call_target="tpu_custom_call" | custom-call | flops 8000000000 | bytes 14000000 | tf_op jit(solution)/shard_map/attn_fwd/pallas_call | solution.py:139
  130.3 64.4 %ffn.1 = (bf16[1024,768]{1,0:T(8,128)(2,1)}, f32[1024,768]{1,0:T(8,128)}, bf16[1024,768]{1,0:T(8,128)(2,1)}, f32[16,768]{1,0:T(8,128)}, f32[16,128]{1,0:T(8,128)}, /*index=5*/bf16[9984,768]{1,0:T(8,128)(2,1)}) custom-call(s32[4]{0:T(128)} %copy-done.7, s32[2]{0:T(128)} %labels.1, s32[2]{0:T(128)} %exits.1, f32[1]{0:T(128)} %bitcast.4.count, f32[3]{0:T(128)} %cls.1, ...), custom_call_target="tpu_custom_call" | custom-call | flops 32999999488 | bytes 40000000 | tf_op jit(solution)/shard_map/ffn/pallas_call | solution.py:274
  194.8 38.4 %attn_bwd.1 = (bf16[2,512,768]{2,1,0:T(8,128)(2,1)}, f32[8,768]{1,0:T(8,128)}, bf16[9984,768]{1,0:T(8,128)(2,1)}) custom-call(s32[4]{0:T(128)} %copy-done.7, s32[2]{0:T(128)} %lens.3, bf16[2,512,768]{2,1,0:T(8,128)(2,1)} %x_ref.3, bf16[2,512,2304]{2,1,0:T(8,128)(2,1)} %get-tuple-element.68.qkv_ref, ...), custom_call_target="tpu_custom_call", output_to_operand_aliasing={{2}: (52, {})} | custom-call | flops 16000000000 | bytes 24000000 | tf_op jit(solution)/shard_map/attn_bwd/pallas_call | solution.py:343
  233.2 3.7 %dynamic-slice_bitcast_fusion.7 = (bf16[624,768]{1,0:T(8,128)(2,1)S(1)}, bf16[624,768]{1,0:T(8,128)(2,1)S(1)}, bf16[624,768]{1,0:T(8,128)(2,1)S(1)}, bf16[624,76...) fusion(bf16[4,2,2,624,768]{4,3,2,1,0:T(8,128)(2,1)} %bitcast.57, ...), kind=kLoop, calls=%fused_computation.33 | loop fusion | bytes 15335452 | tf_op jit(solution)/shard_map/reshape | solution.py:465
  251.8 3.2 collective-permute-done.50
  256.5 5.8 %fusion.9 = (bf16[624,768]{1,0:T(8,128)(2,1)S(1)}, bf16[624,768]{1,0:T(8,128)(2,1)S(1)}, bf16[624,768]{1,0:T(8,128)(2,1)S(1)}, bf16[624,768]{1,0:T(8,128)(2,1)S(...) fusion(bf16[1248,768]{1,0:T(8,128)(2,1)} %collective-permute-do, ...), kind=kLoop, calls=%fused_computation.23 | loop fusion | flops 15335424 | bytes 23003164 | tf_op jit(solution)/shard_map/convert_element_type | solution.py:444
  265.5 8.3 %collective-permute-done.68 = bf16[304,768]{1,0:T(8,128)(2,1)S(1)} collective-permute-done((bf16[304,768]{1,0:T(8,128)(2,1)S(1)}, bf16[304,768]{1,0:T(8,128)(2,1)S(1)}, u32[]{:S(2)}, u32[]{:S(2)}) %collective-permute-start.68) | collective-permute-done | bytes 466976 | tf_op jit(solution)/shard_map/ppermute | solution.py:361
  286.0 5.0 %collective-permute-done.69 = bf16[304,768]{1,0:T(8,128)(2,1)S(1)} collective-permute-done((bf16[304,768]{1,0:T(8,128)(2,1)S(1)}, bf16[304,768]{1,0:T(8,128)(2,1)S(1)}, u32[]{:S(2)}, u32[]{:S(2)}) %collective-permute-start.69) | collective-permute-done | bytes 466976 | tf_op jit(solution)/shard_map/ppermute | solution.py:361
  294.9 3.5 %collective-permute-done.73 = bf16[152,768]{1,0:T(8,128)(2,1)S(1)} collective-permute-done((bf16[152,768]{1,0:T(8,128)(2,1)S(1)}, bf16[152,768]{1,0:T(8,128)(2,1)S(1)}, u32[]{:S(2)}, u32[]{:S(2)}) %collective-permute-start.73) | collective-permute-done | bytes 233504 | tf_op jit(solution)/shard_map/ppermute | solution.py:361
  302.4 4.6 %collective-permute-done.70 = bf16[304,768]{1,0:T(8,128)(2,1)S(1)} collective-permute-done((bf16[304,768]{1,0:T(8,128)(2,1)S(1)}, bf16[304,768]{1,0:T(8,128)(2,1)S(1)}, u32[]{:S(2)}, u32[]{:S(2)}) %collective-permute-start.70) | collective-permute-done | bytes 466976 | tf_op jit(solution)/shard_map/ppermute | solution.py:361
  318.6 3.5 collective-permute-done.71
  329.0 4.8 %collective-permute-done.64 = bf16[160,768]{1,0:T(8,128)(2,1)} collective-permute-done((bf16[160,768]{1,0:T(8,128)(2,1)}, bf16[160,768]{1,0:T(8,128)(2,1)}, u32[]{:S(2)}, u32[]{:S(2)}) %collective-permute-start.64) | collective-permute-done | bytes 245792 | tf_op jit(solution)/shard_map/ppermute | solution.py:361
  339.8 4.1 %collective-permute-done.79 = bf16[312,768]{1,0:T(8,128)(2,1)S(1)} collective-permute-done((bf16[312,768]{1,0:T(8,128)(2,1)S(1)}, bf16[312,768]{1,0:T(8,128)(2,1)S(1)}, u32[]{:S(2)}, u32[]{:S(2)}) %collective-permute-start.79) | collective-permute-done | bytes 479264 | tf_op jit(solution)/shard_map/ppermute | solution.py:361
  344.0 6.2 %fusion.22 = (bf16[624,768]{1,0:T(8,128)(2,1)}, f32[624,768]{1,0:T(8,128)}, f32[624,768]{1,0:T(8,128)}, f32[624,768]{1,0:T(8,128)}) fusion(f32[624,768]{1,0:T(8,128)S(1)} %copy-done.21, f32[624]{0:T(1024)S(1)} %select_select_fusion, bf16[152,768]{1,0:T(8,128)(2,1)S(1)} %get-tuple-element.130, bf16[152,768]{1,0:T(8,128)(2,1)S(1)} %get-tuple-element.129, ...), kind=kLoop, calls=%fused_computation.110 | loop fusion | flops 11501568 | bytes 13420992 | tf_op jit(solution)/shard_map/convert_element_type | solution.py:600
  (315 shorter events, 114.1 us)
Async XLA Ops:
  2.4 28.0 %collective-permute-start.12 = (bf16[160,768]{1,0:T(8,128)(2,1)S(1)}, bf16[160,768]{1,0:T(8,128)(2,1)S(1)}, u32[]{:S(2)}, u32[]{:S(2)}) collective-permute-start(bf16[160,768]{1,0:T(8,128)(2,1)S(1)} %constant_dynamic-slice_fusion.14), channel_id=1, source_target_pairs={{0,4},{1,5},{2,6},{3,7},{4,8},{5,9},{6,10},{7,11},{8,12},{9,13},{1... | collective-permute-start | bytes 737288 | tf_op jit(solution)/shard_map/ppermute | solution.py:361
  5.4 24.9 %collective-permute-start.6 = (bf16[160,768]{1,0:T(8,128)(2,1)S(1)}, bf16[160,768]{1,0:T(8,128)(2,1)S(1)}, u32[]{:S(2)}, u32[]{:S(2)}) collective-permute-start(bf16[160,768]{1,0:T(8,128)(2,1)S(1)} %constant_dynamic-slice_fusion.14), channel_id=1, source_target_pairs={{0,2},{1,3},{2,0},{3,1},{4,6},{5,7},{6,4},{7,5},{8,10},{9,11},{10,... | collective-permute-start | bytes 737288 | tf_op jit(solution)/shard_map/ppermute | solution.py:361
  7.0 27.4 %collective-permute-start.8 = (bf16[304,768]{1,0:T(8,128)(2,1)S(1)}, bf16[304,768]{1,0:T(8,128)(2,1)}, u32[]{:S(2)}, u32[]{:S(2)}) collective-permute-start(bf16[304,768]{1,0:T(8,128)(2,1)S(1)} %slice.139), channel_id=1, source_target_pairs={{0,2},{1,3},{2,0},{3,1},{4,6},{5,7},{6,4},{7,5},{8,10},{9,11},{10,... | collective-permute-start | bytes 1400840 | tf_op jit(solution)/shard_map/ppermute | solution.py:361
  10.6 21.7 %collective-permute-start.14 = (bf16[160,768]{1,0:T(8,128)(2,1)S(1)}, bf16[160,768]{1,0:T(8,128)(2,1)S(1)}, u32[]{:S(2)}, u32[]{:S(2)}) collective-permute-start(bf16[160,768]{1,0:T(8,128)(2,1)S(1)} %constant_dynamic-slice_fusion.13), channel_id=1, source_target_pairs={{0,4},{1,5},{2,6},{3,7},{4,8},{5,9},{6,10},{7,11},{8,12},{9,13},{1... | collective-permute-start | bytes 737288 | tf_op jit(solution)/shard_map/ppermute | solution.py:361
  43.4 15.6 %collective-permute-start.22 = (bf16[320,768]{1,0:T(8,128)(2,1)S(1)}, bf16[320,768]{1,0:T(8,128)(2,1)}, u32[]{:S(2)}, u32[]{:S(2)}) collective-permute-start(bf16[320,768]{1,0:T(8,128)(2,1)S(1)} %pad_maximum_fusion.6), channel_id=1, source_target_pairs={{0,2},{1,3},{2,0},{3,1},{4,6},{5,7},{6,4},{7,5},{8,10},{9,11},{10,... | collective-permute-start | bytes 1474568 | tf_op jit(solution)/shard_map/ppermute | solution.py:361
  50.6 17.9 %collective-permute-start.20 = (bf16[320,768]{1,0:T(8,128)(2,1)S(1)}, bf16[320,768]{1,0:T(8,128)(2,1)S(1)}, u32[]{:S(2)}, u32[]{:S(2)}) collective-permute-start(bf16[320,768]{1,0:T(8,128)(2,1)S(1)} %pad_maximum_fusion.5), channel_id=1, source_target_pairs={{0,16},{16,0},{1,17},{17,1},{2,18},{18,2},{3,19},{19,3},{4,20},{20... | collective-permute-start | bytes 1474568 | tf_op jit(solution)/shard_map/ppermute | solution.py:361
  55.4 12.8 %collective-permute-start.30 = (bf16[160,768]{1,0:T(8,128)(2,1)S(1)}, bf16[160,768]{1,0:T(8,128)(2,1)S(1)}, u32[]{:S(2)}, u32[]{:S(2)}) collective-permute-start(bf16[160,768]{1,0:T(8,128)(2,1)S(1)} %collective-permute-done.26.refs_22_), channel_id=1, source_target_pairs={{0,16},{16,0},{1,17},{17,1},{2,18},{18,2},{3,19},{19,3},{4,20},{20... | collective-permute-start | bytes 737288 | tf_op jit(solution)/shard_map/ppermute | solution.py:361
  56.9 21.5 %collective-permute-start.9 = (bf16[304,768]{1,0:T(8,128)(2,1)}, bf16[304,768]{1,0:T(8,128)(2,1)}, u32[]{:S(2)}, u32[]{:S(2)}) collective-permute-start(bf16[304,768]{1,0:T(8,128)(2,1)} %collective-permute-done.8.refs_4_), channel_id=1, source_target_pairs={{0,1},{1,0},{2,3},{3,2},{4,5},{5,4},{6,7},{7,6},{8,9},{9,8},{10,11... | collective-permute-start | bytes 1400840 | tf_op jit(solution)/shard_map/ppermute | solution.py:361
  59.0 33.6 %collective-permute-start.5 = (bf16[624,768]{1,0:T(8,128)(2,1)S(1)}, bf16[624,768]{1,0:T(8,128)(2,1)S(1)}, u32[]{:S(2)}, u32[]{:S(2)}) collective-permute-start(bf16[624,768]{1,0:T(8,128)(2,1)S(1)} %copy-done.23), channel_id=1, source_target_pairs={{0,1},{1,0},{2,3},{3,2},{4,5},{5,4},{6,7},{7,6},{8,9},{9,8},{10,11... | collective-permute-start | bytes 2875400 | tf_op jit(solution)/shard_map/ppermute | solution.py:361
  68.5 23.4 %collective-permute-start.34 = (bf16[320,768]{1,0:T(8,128)(2,1)S(1)}, bf16[320,768]{1,0:T(8,128)(2,1)}, u32[]{:S(2)}, u32[]{:S(2)}) collective-permute-start(bf16[320,768]{1,0:T(8,128)(2,1)S(1)} %pad_maximum_fusion.8), channel_id=1, source_target_pairs={{0,2},{1,3},{2,0},{3,1},{4,6},{5,7},{6,4},{7,5},{8,10},{9,11},{10,... | collective-permute-start | bytes 1474568 | tf_op jit(solution)/shard_map/ppermute | solution.py:361
  76.3 16.1 %collective-permute-start.32 = (bf16[320,768]{1,0:T(8,128)(2,1)S(1)}, bf16[320,768]{1,0:T(8,128)(2,1)}, u32[]{:S(2)}, u32[]{:S(2)}) collective-permute-start(bf16[320,768]{1,0:T(8,128)(2,1)S(1)} %pad_maximum_fusion.7), channel_id=1, source_target_pairs={{0,16},{16,0},{1,17},{17,1},{2,18},{18,2},{3,19},{19,3},{4,20},{20... | collective-permute-start | bytes 1474568 | tf_op jit(solution)/shard_map/ppermute | solution.py:361
  78.4 13.5 %collective-permute-start.42 = (bf16[160,768]{1,0:T(8,128)(2,1)S(1)}, bf16[160,768]{1,0:T(8,128)(2,1)S(1)}, u32[]{:S(2)}, u32[]{:S(2)}) collective-permute-start(bf16[160,768]{1,0:T(8,128)(2,1)S(1)} %collective-permute-done.38.refs_34_), channel_id=1, source_target_pairs={{0,16},{16,0},{1,17},{17,1},{2,18},{18,2},{3,19},{19,3},{4,20},{20... | collective-permute-start | bytes 737288 | tf_op jit(solution)/shard_map/ppermute | solution.py:361
  94.1 13.5 %collective-permute-start.46 = (bf16[320,768]{1,0:T(8,128)(2,1)S(1)}, bf16[320,768]{1,0:T(8,128)(2,1)}, u32[]{:S(2)}, u32[]{:S(2)}) collective-permute-start(bf16[320,768]{1,0:T(8,128)(2,1)S(1)} %pad_maximum_fusion.10), channel_id=1, source_target_pairs={{0,2},{1,3},{2,0},{3,1},{4,6},{5,7},{6,4},{7,5},{8,10},{9,11},{10,... | collective-permute-start | bytes 1474568 | tf_op jit(solution)/shard_map/ppermute | solution.py:361
  94.7 13.2 %collective-permute-start.44 = (bf16[320,768]{1,0:T(8,128)(2,1)S(1)}, bf16[320,768]{1,0:T(8,128)(2,1)}, u32[]{:S(2)}, u32[]{:S(2)}) collective-permute-start(bf16[320,768]{1,0:T(8,128)(2,1)S(1)} %pad_maximum_fusion.9), channel_id=1, source_target_pairs={{0,16},{16,0},{1,17},{17,1},{2,18},{18,2},{3,19},{19,3},{4,20},{20... | collective-permute-start | bytes 1474568 | tf_op jit(solution)/shard_map/ppermute | solution.py:361
  238.3 18.2 %collective-permute-start.54 = (bf16[1248,768]{1,0:T(8,128)(2,1)}, bf16[1248,768]{1,0:T(8,128)(2,1)S(1)}, u32[]{:S(2)}, u32[]{:S(2)}) collective-permute-start(bf16[1248,768]{1,0:T(8,128)(2,1)} %pad_maximum_fusion.1), channel_id=1, source_target_pairs={{0,1},{1,0},{2,3},{3,2},{4,5},{5,4},{6,7},{7,6},{8,9},{9,8},{10,11... | collective-permute-start | bytes 5750792 | tf_op jit(solution)/shard_map/ppermute | solution.py:361
  239.8 16.7 %collective-permute-start.55 = (bf16[1248,768]{1,0:T(8,128)(2,1)}, bf16[1248,768]{1,0:T(8,128)(2,1)}, u32[]{:S(2)}, u32[]{:S(2)}) collective-permute-start(bf16[1248,768]{1,0:T(8,128)(2,1)} %pad_maximum_fusion.2), channel_id=1, source_target_pairs={{0,1},{1,0},{2,3},{3,2},{4,5},{5,4},{6,7},{7,6},{8,9},{9,8},{10,11... | collective-permute-start | bytes 5750792 | tf_op jit(solution)/shard_map/ppermute | solution.py:361
  241.6 14.9 %collective-permute-start.56 = (bf16[1248,768]{1,0:T(8,128)(2,1)}, bf16[1248,768]{1,0:T(8,128)(2,1)}, u32[]{:S(2)}, u32[]{:S(2)}) collective-permute-start(bf16[1248,768]{1,0:T(8,128)(2,1)} %pad_maximum_fusion.3), channel_id=1, source_target_pairs={{0,1},{1,0},{2,3},{3,2},{4,5},{5,4},{6,7},{7,6},{8,9},{9,8},{10,11... | collective-permute-start | bytes 5750792 | tf_op jit(solution)/shard_map/ppermute | solution.py:361
  243.1 13.4 %collective-permute-start.53 = (bf16[1248,768]{1,0:T(8,128)(2,1)}, bf16[1248,768]{1,0:T(8,128)(2,1)}, u32[]{:S(2)}, u32[]{:S(2)}) collective-permute-start(bf16[1248,768]{1,0:T(8,128)(2,1)} %pad_maximum_fusion), channel_id=1, source_target_pairs={{0,1},{1,0},{2,3},{3,2},{4,5},{5,4},{6,7},{7,6},{8,9},{9,8},{10,11... | collective-permute-start | bytes 5750792 | tf_op jit(solution)/shard_map/ppermute | solution.py:361
  255.0 73.4 %collective-permute-start.51 = (f32[24,768]{1,0:T(8,128)S(1)}, f32[24,768]{1,0:T(8,128)S(1)}, u32[]{:S(2)}, u32[]{:S(2)}) collective-permute-start(f32[24,768]{1,0:T(8,128)S(1)} %add.338), channel_id=1, source_target_pairs={{0,4},{1,5},{2,6},{3,7},{4,0},{5,1},{6,2},{7,3},{8,12},{9,13},{10,... | collective-permute-start | bytes 221192 | tf_op jit(solution)/shard_map/ppermute | solution.py:361
  277.0 14.1 %collective-permute-start.69 = (bf16[304,768]{1,0:T(8,128)(2,1)S(1)}, bf16[304,768]{1,0:T(8,128)(2,1)S(1)}, u32[]{:S(2)}, u32[]{:S(2)}) collective-permute-start(bf16[304,768]{1,0:T(8,128)(2,1)S(1)} %slice.160), channel_id=1, source_target_pairs={{0,2},{1,3},{2,0},{3,1},{4,6},{5,7},{6,4},{7,5},{8,10},{9,11},{10,... | collective-permute-start | bytes 1400840 | tf_op jit(solution)/shard_map/ppermute | solution.py:361
  278.6 14.0 %collective-permute-start.58 = (bf16[320,768]{1,0:T(8,128)(2,1)S(1)}, bf16[320,768]{1,0:T(8,128)(2,1)S(1)}, u32[]{:S(2)}, u32[]{:S(2)}) collective-permute-start(bf16[320,768]{1,0:T(8,128)(2,1)S(1)} %pad_maximum_fusion.13), channel_id=1, source_target_pairs={{0,16},{16,0},{1,17},{17,1},{2,18},{18,2},{3,19},{19,3},{4,20},{20... | collective-permute-start | bytes 1474568 | tf_op jit(solution)/shard_map/ppermute | solution.py:361
  285.4 14.3 %collective-permute-start.65 = (bf16[160,768]{1,0:T(8,128)(2,1)S(1)}, bf16[160,768]{1,0:T(8,128)(2,1)S(1)}, u32[]{:S(2)}, u32[]{:S(2)}) collective-permute-start(bf16[160,768]{1,0:T(8,128)(2,1)S(1)} %add_convert_fusion.7), channel_id=1, source_target_pairs={{0,4},{1,5},{2,6},{3,7},{4,8},{5,9},{6,10},{7,11},{8,12},{9,13},{1... | collective-permute-start | bytes 737288 | tf_op jit(solution)/shard_map/ppermute | solution.py:361
  293.7 13.4 %collective-permute-start.70 = (bf16[304,768]{1,0:T(8,128)(2,1)S(1)}, bf16[304,768]{1,0:T(8,128)(2,1)S(1)}, u32[]{:S(2)}, u32[]{:S(2)}) collective-permute-start(bf16[304,768]{1,0:T(8,128)(2,1)S(1)} %slice.159), channel_id=1, source_target_pairs={{0,2},{1,3},{2,0},{3,1},{4,6},{5,7},{6,4},{7,5},{8,10},{9,11},{10,... | collective-permute-start | bytes 1400840 | tf_op jit(solution)/shard_map/ppermute | solution.py:361
  301.8 14.6 %collective-permute-start.66 = (bf16[160,768]{1,0:T(8,128)(2,1)S(1)}, bf16[160,768]{1,0:T(8,128)(2,1)S(1)}, u32[]{:S(2)}, u32[]{:S(2)}) collective-permute-start(bf16[160,768]{1,0:T(8,128)(2,1)S(1)} %add_convert_fusion.6), channel_id=1, source_target_pairs={{0,4},{1,5},{2,6},{3,7},{4,8},{5,9},{6,10},{7,11},{8,12},{9,13},{1... | collective-permute-start | bytes 737288 | tf_op jit(solution)/shard_map/ppermute | solution.py:361
  (105 other events, 1959.2 us)

commit v2 on v1

--- a/solution.py
+++ b/solution.py
@@ -26,8 +26,11 @@
 def dot(a, b, dims=NN):
     return lax.dot_general(a, b, dims, preferred_element_type=f32)
 ANY = pl.BlockSpec(memory_space=pl.ANY)
+VMEM = pl.BlockSpec(memory_space=pltpu.VMEM)
 HBM = pl.BlockSpec(memory_space=pltpu.HBM)
 MROWS = 5 * D + 2 * FF
+EARLY = 128
+CHUNK = 384
 SMEM = pl.BlockSpec(memory_space=pltpu.SMEM)
 TILE = 256
 R = 16
@@ -48,7 +51,7 @@
             else:
                 shard, at = plan.locate(row, place)
                 cond = (shard * plan.rows >= low) & (shard * plan.rows < high)
-                source = refs[piece].at[pl.ds(plan.skip(src, row, place), count)]
+                source = refs[piece].at[pl.ds(src, count)]
                 target = dst.at[pl.ds(pl.multiple_of(jnp.where(cond, at - low, 0), 16), count)]
             self.items.append((cond, pltpu.make_async_copy(source, target, sems.at[j])))
 
@@ -68,9 +71,8 @@
 
 
 class Plan:
-    def __init__(self, spans, rows, first=0):
-        self.spans, self.rows, self.first = spans, rows, first
-        self.part_e = -(-(rows // 2 - first) // 16) * 16
+    def __init__(self, spans, rows, parts=(0, 0, 0)):
+        self.spans, self.rows, self.parts = spans, rows, parts
         self.head_end = -(-3 * D // rows) * rows
         self.tail_start = 3 * D // rows * rows
 
@@ -79,22 +81,56 @@
         z, x, core, rep = (place[i] for i in range(4))
         flip = lambda bit, other: 1 - bit if other else bit
         shard = (lax.rem(z - steps + 4, 4) * 2 + flip(x, other_x)) * 2 + flip(core, other_core)
-        low_e = 2 * self.first
-        part_e, size_e = self.part_e, self.rows - low_e
+        a, c, e = self.parts
         base = {
             "all": 0,
-            "e": low_e,
-            "c_mine": rep * self.first,
-            "c_other": (1 - rep) * self.first,
-            "e_mine": low_e + rep * (size_e - part_e),
-            "e_other": low_e + (1 - rep) * part_e,
+            "a": 0,
+            "c_mine": a + rep * c,
+            "c_other": a + (1 - rep) * c,
+            "e": a + 2 * c,
+            "e_late": a + 2 * c + EARLY,
+            "e_mine": a + 2 * c + rep * e,
+            "e_other": a + 2 * c + (1 - rep) * e,
         }[part]
         return shard, shard * self.rows + base
 
-    def skip(self, start, where, place):
-        if where[3] != "e_other":
-            return start
-        return pl.multiple_of(start + (1 - place[3]) * (2 * (self.first + self.part_e) - self.rows), 16)
+
+class Layout:
+    def __init__(self, rows, half):
+        self.rows, self.half = rows, half
+        self.shapes = [jax.ShapeDtypeStruct((2 * rows, D), bf16)] * 8 if half else [jax.ShapeDtypeStruct((MROWS, D), bf16)]
+
+    def write(self, place, staged, low, targets, sem, first, count):
+        def start(target, at, rows, row):
+            pltpu.make_async_copy(staged.at[pl.ds(at - low, rows)], target.at[pl.ds(row, rows)], sem).start()
+
+        if not self.half:
+            start(targets[0], first, count, first)
+            return
+        z, x, core, rep = (place[i] for i in range(4))
+        rows, half = self.rows, self.half
+        for shard in range(first // rows, -(-(first + count) // rows)):
+            far_x, far_core = jnp.abs(x - shard // 2 % 2), jnp.abs(core - shard % 2)
+            group = far_core * 4 + lax.rem(z - shard // 4 + 4, 4)
+            runs = (
+                (0, half, rep * 2 * half + far_x * half),
+                (half, half, (1 - rep) * 2 * half + far_x * half),
+                (2 * half, rows - 2 * half, 4 * half + (1 - far_x) * (rows - 2 * half)),
+            )
+
+            def put(target, shard=shard, runs=runs):
+                for inner, size, row in runs:
+                    begin = max(first, shard * rows + inner)
+                    end = min(first + count, shard * rows + inner + size)
+                    if begin < end:
+                        start(target, begin, end - begin, pl.multiple_of(row + begin - shard * rows - inner, 16))
+
+            for index, target in enumerate(targets):
+                pl.when(group == index)(functools.partial(put, target))
+
+    def wait(self, staged, low, targets, sem, first, count):
+        rows = staged.at[pl.ds(first - low, count)]
+        pltpu.make_async_copy(rows, rows, sem).wait()
 
 
 def attn_fwd_kernel(plan, n, place, lens, x_ref, vec_ref, *refs):
@@ -166,9 +202,11 @@
     g = u * phi
     return g, phi + (u * bell) * (2 * math.pi) ** -0.5
 
-def ffn_kernel(plan, n, tiles, low, place, labels, exits, count, cls, x_ref, c_ref, og_ref, vec_ref, *refs):
-    pieces = refs[:n]
-    out_ref, dh1_ref, dc_ref, vg_ref, sc_ref, gw_ref, w, sems, g_s, du_s, n1_s, df_s, da_s, cc_s, gp_s, dy_s, e_s, z_s, stage, osem = refs[n:]
+def ffn_kernel(plan, layout, n, tiles, low, place, labels, exits, count, cls, x_ref, c_ref, og_ref, vec_ref, *refs):
+    m = n + 5 + len(layout.shapes)
+    pieces, gw_refs = refs[:n], refs[n + 5:m]
+    out_ref, dh1_ref, dc_ref, vg_ref, sc_ref = refs[n:n + 5]
+    w, sems, g_s, du_s, n1_s, df_s, da_s, cc_s, gp_s, dy_s, e_s, z_s, osem = refs[m:]
     i = pl.program_id(0)
     ld = Loads(plan, pieces, place, w, sems, low, MROWS)
     @pl.when(i == 0)
@@ -248,44 +286,39 @@
     dc_ref[...] = dot(dab, w[wo:wo + D], NT).astype(bf16)
     @pl.when(i == tiles - 1)
     def _():
-        C = 384
-        def flush(slot, base):
-            return pltpu.make_async_copy(stage.at[slot], gw_ref.at[pl.ds(base, C)], osem.at[slot])
-        stage[0] = dot(e_s[:, 0:C], z_s[...], TN).astype(bf16); flush(0, 4 * D).start()
-        stage[1] = dot(e_s[:, C:2 * C], z_s[...], TN).astype(bf16); flush(1, 4 * D + C).start()
-        def grads(lhs, rhs, width, base):
-            def step(r, _):
-                slot = lax.rem(r, 2)
-                at = pl.multiple_of(r * C, C)
-                v = dot(lhs[:, pl.ds(at, C)], rhs[...], TN).astype(bf16)
-                flush(slot, base).wait()
-                stage[slot] = v
-                flush(slot, pl.multiple_of(base + at, C)).start()
-                return 0
-            lax.fori_loop(0, width // C, step, 0)
-        grads(cc_s, da_s, D, 3 * D)
-        grads(du_s, n1_s, FF, 5 * D)
-        grads(g_s, df_s, FF, 5 * D + FF)
-        flush(0, 0).wait(); flush(1, 0).wait()
-
-def ffn(plan, pieces, place, labels, exits, count, cls, x, ctx, og, vec, total):
+        for lhs, rhs, width, base in ((e_s, z_s, D, 4 * D), (cc_s, da_s, D, 3 * D), (du_s, n1_s, FF, 5 * D), (g_s, df_s, FF, 5 * D + FF)):
+
+            def step(r, carry, lhs=lhs, rhs=rhs, base=base):
+                at = pl.multiple_of(r * CHUNK, CHUNK)
+                w[pl.ds(pl.multiple_of(base - low + at, 16), CHUNK)] = dot(lhs[:, pl.ds(at, CHUNK)], rhs[...], TN).astype(bf16)
+                return carry
+
+            lax.fori_loop(0, width // CHUNK, step, 0)
+            layout.write(place, w, low, gw_refs, osem.at[0], base, width)
+        layout.wait(w, low, gw_refs, osem.at[0], 3 * D, MROWS - 3 * D)
+
+def ffn(plan, layout, pieces, place, labels, exits, count, cls, x, ctx, og, vec):
     n = len(pieces); T = x.shape[0]; tiles = T // TILE; low = plan.tail_start
     tok = lambda dt: pl.BlockSpec((TILE, D), lambda i: (i, 0))
     return pl.pallas_call(
-        functools.partial(ffn_kernel, plan, n, tiles, low), grid=(tiles,), name="ffn",
+        functools.partial(ffn_kernel, plan, layout, n, tiles, low), grid=(tiles,), name="ffn",
         in_specs=[SMEM] * 5 + [tok(0)] * 3 + [pl.BlockSpec((16, D), lambda i: (0, 0))] + [HBM] * n,
-        out_specs=[tok(0), tok(0), tok(0), pl.BlockSpec((16, D), lambda i: (0, 0)), pl.BlockSpec((R, 128), lambda i: (0, 0)), ANY],
-        out_shape=[jax.ShapeDtypeStruct((T, D), bf16), jax.ShapeDtypeStruct((T, D), f32), jax.ShapeDtypeStruct((T, D), bf16), jax.ShapeDtypeStruct((16, D), f32), jax.ShapeDtypeStruct((R, 128), f32), jax.ShapeDtypeStruct((total, D), bf16)],
+        out_specs=[tok(0), tok(0), tok(0), pl.BlockSpec((16, D), lambda i: (0, 0)), pl.BlockSpec((R, 128), lambda i: (0, 0))] + [ANY] * len(layout.shapes),
+        out_shape=[jax.ShapeDtypeStruct((T, D), bf16), jax.ShapeDtypeStruct((T, D), f32), jax.ShapeDtypeStruct((T, D), bf16), jax.ShapeDtypeStruct((16, D), f32), jax.ShapeDtypeStruct((R, 128), f32)] + layout.shapes,
         scratch_shapes=[pltpu.VMEM((MROWS - low, D), bf16), pltpu.SemaphoreType.DMA((len(plan.spans),)),
             pltpu.VMEM((T, FF), bf16), pltpu.VMEM((T, FF), bf16), pltpu.VMEM((T, D), bf16), pltpu.VMEM((T, D), bf16), pltpu.VMEM((T, D), bf16), pltpu.VMEM((T, D), bf16),
             pltpu.VMEM((TILE, FF), f32), pltpu.VMEM((TILE, D), f32), pltpu.VMEM((R * (T // L), D), bf16), pltpu.VMEM((R * (T // L), D), bf16),
-            pltpu.VMEM((2, 384, D), bf16), pltpu.SemaphoreType.DMA((2,))],
+            pltpu.SemaphoreType.DMA((1,))],
         compiler_params=pltpu.CompilerParams(vmem_limit_bytes=60 << 20),
         cost_estimate=pl.CostEstimate(flops=33 * 10 ** 9, bytes_accessed=40 * 10 ** 6, transcendentals=6 * 10 ** 6),
     )(place, labels, exits, count, cls, x, ctx, og, vec, *pieces)
 
-def attn_bwd_kernel(plan, n, S, place, lens, x_ref, qkv_ref, dc_ref, c_ref, st_ref, dh1_ref, *refs):
-    pieces = refs[:n]; gw_in, dx_ref, vg_ref, gw_ref, w, sems, d_s, x_s, stage, osem = refs[n:]
+def attn_bwd_kernel(plan, layout, n, S, place, lens, x_ref, qkv_ref, dc_ref, c_ref, st_ref, dh1_ref, *refs):
+    m = len(layout.shapes)
+    pieces = refs[:n]
+    dx_ref, vg_ref = refs[n + m:n + m + 2]
+    gw_refs = refs[n + m + 2:n + 2 * m + 2]
+    w, sems, d_s, x_s, osem = refs[n + 2 * m + 2:]
     s = pl.program_id(0)
     ld = Loads(plan, pieces, place, w, sems, 0, plan.head_end)
     @pl.when(s == 0)
@@ -326,62 +359,46 @@
     vg_ref[1:2] += jnp.sum(dv.astype(f32), axis=0, keepdims=True)
     @pl.when(s == S - 1)
     def _():
-        C = 384
-        def flush(slot, base):
-            return pltpu.make_async_copy(stage.at[slot], gw_ref.at[pl.ds(base, C)], osem.at[slot])
         for i in range(3):
-            for r in range(2):
-                v = dot(x_s[:, r * C:(r + 1) * C], d_s[:, i * D:(i + 1) * D], TN).astype(bf16)
-                if i: flush(r, 0).wait()
-                stage[r] = v
-                flush(r, i * D + r * C).start()
-        flush(0, 0).wait(); flush(1, 0).wait()
-
-def attn_bwd(plan, pieces, place, lengths, tokens, qkv, dc, ctx, st, dh1, gw):
-    n = len(pieces); S = tokens.shape[0]
+            for at in range(0, D, CHUNK):
+                w[i * D + at:i * D + at + CHUNK] = dot(x_s[:, at:at + CHUNK], d_s[:, i * D:(i + 1) * D], TN).astype(bf16)
+            layout.write(place, w, 0, gw_refs, osem.at[0], i * D, D)
+        layout.wait(w, 0, gw_refs, osem.at[0], 0, 3 * D)
+
+def attn_bwd(plan, layout, pieces, place, lengths, tokens, qkv, dc, ctx, st, dh1, gw):
+    n, m, S = len(pieces), len(gw), tokens.shape[0]
     seq = lambda *sh: pl.BlockSpec((1,) + sh, lambda s: (s, 0, 0))
     return pl.pallas_call(
-        functools.partial(attn_bwd_kernel, plan, n, S), grid=(S,), name="attn_bwd",
-        in_specs=[SMEM, SMEM, seq(L, D), seq(L, 3 * D), seq(L, D), seq(L, D), seq(128, L), seq(L, D)] + [HBM] * n + [ANY],
-        out_specs=[seq(L, D), pl.BlockSpec((8, D), lambda s: (0, 0)), ANY],
-        out_shape=[jax.ShapeDtypeStruct((S, L, D), bf16), jax.ShapeDtypeStruct((8, D), f32), jax.ShapeDtypeStruct(gw.shape, bf16)],
-        input_output_aliases={8 + n: 2},
-        scratch_shapes=[pltpu.VMEM((plan.head_end, D), bf16), pltpu.SemaphoreType.DMA((len(plan.spans),)), pltpu.VMEM((S * L, 3 * D), bf16), pltpu.VMEM((S * L, D), bf16), pltpu.VMEM((2, 384, D), bf16), pltpu.SemaphoreType.DMA((2,))],
+        functools.partial(attn_bwd_kernel, plan, layout, n, S), grid=(S,), name="attn_bwd",
+        in_specs=[SMEM, SMEM, seq(L, D), seq(L, 3 * D), seq(L, D), seq(L, D), seq(128, L), seq(L, D)] + [HBM] * n + [ANY] * m,
+        out_specs=[seq(L, D), pl.BlockSpec((8, D), lambda s: (0, 0))] + [ANY] * m,
+        out_shape=[jax.ShapeDtypeStruct((S, L, D), bf16), jax.ShapeDtypeStruct((8, D), f32)] + layout.shapes,
+        input_output_aliases={8 + n + i: 2 + i for i in range(m)},
+        scratch_shapes=[pltpu.VMEM((plan.head_end, D), bf16), pltpu.SemaphoreType.DMA((len(plan.spans),)), pltpu.VMEM((S * L, 3 * D), bf16), pltpu.VMEM((S * L, D), bf16), pltpu.SemaphoreType.DMA((1,))],
         compiler_params=pltpu.CompilerParams(vmem_limit_bytes=56 << 20),
         cost_estimate=pl.CostEstimate(flops=16 * 10 ** 9, bytes_accessed=24 * 10 ** 6, transcendentals=6 * 10 ** 6),
-    )(place, lengths, tokens, qkv, dc, ctx, st, dh1, *pieces, gw)
+    )(place, lengths, tokens, qkv, dc, ctx, st, dh1, *pieces, *gw)
 
 
 FSDP = 16
 
 
-def permute(axis, pairs, value, after):
-    if after:
-        value = lax.optimization_barrier((value, *after))[0]
-    return lax.ppermute(value, axis, pairs)
-
-
-def swap_core(value, *after):
-    return permute("fsdp", [(i, i ^ 1) for i in range(FSDP)], value, after)
-
-
-def swap_x(value, *after):
-    return permute("fsdp", [(i, i ^ 2) for i in range(FSDP)], value, after)
-
-
-def swap_y(value, *after):
-    return permute("dp", [(0, 1), (1, 0)], value, after)
-
-
-def next_z(value, *after):
-    return permute("fsdp", [(i, (i + 4) % FSDP) for i in range(FSDP)], value, after)
-
-
-def sum_small(value):
-    value = value + swap_y(value)
-    for bit in (1, 2, 4, 8):
-        value = value + permute("fsdp", [(i, i ^ bit) for i in range(FSDP)], value, ())
-    return value
+WAYS = {
+    "x": ("fsdp", tuple((i, i ^ 2) for i in range(FSDP))),
+    "y": ("dp", ((0, 1), (1, 0))),
+    "z": ("fsdp", tuple((i, (i + 4) % FSDP) for i in range(FSDP))),
+    "core": ("fsdp", tuple((i, i ^ 1) for i in range(FSDP))),
+}
+PARTS = (80, 128, 144)
+HALF = 160
+
+
+def hold(value, *others):
+    return lax.optimization_barrier((value, *others))[0] if others else value
+
+
+def send(way, *values):
+    return lax.ppermute(values[0] if len(values) == 1 else jnp.concatenate(values), *WAYS[way])
 
 
 def position():
@@ -389,99 +406,116 @@
     return index // 4, index // 2 % 2, index % 2, lax.axis_index("dp")
 
 
-def gather_pieces(shard, first):
-    rows = shard.shape[0]
-    plan = Plan([], rows, first)
-    c, e, spans = first, plan.part_e, plan.spans
-    size_e = rows - 2 * c
-    rep = lax.axis_index("dp")
-    low_e = shard[2 * c :]
-    my_c = lax.dynamic_slice_in_dim(shard, rep * c, c)
-    my_e = lax.dynamic_slice_in_dim(low_e, rep * (size_e - e), e)
-    x0c, x0e = swap_x(my_c), swap_x(low_e)
-    zc1, ze1 = next_z(my_c), next_z(my_e)
-    ye1 = swap_y(ze1)
-    xc1 = swap_x(zc1, x0c)
-    zc2 = next_z(zc1, x0c)
-    ze2 = next_z(ze1, x0e)
-    y0 = swap_y(x0c)
-    xe1 = swap_x(jnp.concatenate([ze1, ye1]), x0e)
-    yc1 = swap_y(jnp.concatenate([zc1, xc1]))
-    ye2 = swap_y(ze2, y0)
-    xc2 = swap_x(zc2, xc1)
-    zc3 = next_z(zc2, xc1)
-    ze3 = next_z(ze2, xe1)
-    xe2 = swap_x(jnp.concatenate([ze2, ye2]), xe1)
-    ye3 = swap_y(ze3, yc1)
-    yc2 = swap_y(jnp.concatenate([zc2, xc2]), yc1)
-    xc3 = swap_x(zc3, xc2)
-    xe3 = swap_x(jnp.concatenate([ze3, ye3]), xe2)
-    yc3 = swap_y(jnp.concatenate([zc3, xc3]), yc2)
-    pieces = []
-
-    def both(value, *parts):
-        for other_core, piece in ((0, value), (1, swap_core(value))):
+def gather(shard, small):
+    a, c, e = PARTS
+    rows, rep = shard.shape[0], lax.axis_index("dp")
+    cut = lax.dynamic_slice_in_dim
+    all_a, all_e = shard[:a], shard[a + 2 * c :]
+    my_c, my_e = cut(shard, a + rep * c, c), cut(shard, a + 2 * c + rep * e, e)
+    late = 2 * e - EARLY
+    zc, ze = (lambda k: z[k][:c]), (lambda k: z[k][c : c + e])
+    z, za = {}, {}
+    z[1] = send("z", my_c, my_e, small)
+    x1 = send("x", all_a, my_c, all_e[:EARLY])
+    z[2] = send("z", z[1])
+    x2 = send("x", all_e[EARLY:], zc(1))
+    y2 = send("y", x1[a : a + c], ze(1))
+    za[1] = send("z", all_a, x1[:a])
+    x3 = send("x", zc(2), ze(1), y2[c:])
+    y3 = send("y", zc(1), x2[late:], ze(2))
+    z[3] = send("z", hold(z[2], x2))
+    za[2] = send("z", hold(za[1], y2, x2))
+    small = small + z[1][c + e :] + z[2][c + e :] + z[3][c + e :]
+    x4 = send("x", zc(3), ze(2), y3[2 * c :], small)
+    y4 = send("y", zc(2), x3[:c], ze(3))
+    za[3] = send("z", hold(za[2], y3, x3))
+    small = small + x4[c + 2 * e :]
+    x5 = send("x", ze(3), y4[2 * c :])
+    y5 = send("y", zc(3), x4[:c], small)
+    small = small + y5[2 * c :]
+    za = {1: hold(za[1], x3, y3), 2: hold(za[2], x4, y4), 3: hold(za[3], x5, y5)}
+    small = small + send("core", small)
+    held = [(shard, ((0, rows, 0, 0, "all"),))]
+    for k in (1, 2, 3):
+        held.append((z[k], ((0, c, k, 0, "c_mine"), (c, e, k, 0, "e_mine"))))
+        held.append((za[k], ((0, a, k, 0, "a"), (a, a, k, 1, "a"))))
+    held.append((x1, ((0, a, 0, 1, "a"), (a, c, 0, 1, "c_mine"), (a + c, EARLY, 0, 1, "e"))))
+    held.append((x2, ((0, late, 0, 1, "e_late"), (late, c, 1, 1, "c_mine"))))
+    held.append((y2, ((0, c, 0, 1, "c_other"), (c, e, 1, 0, "e_other"))))
+    for k, x_got, y_got in ((2, x3, y3), (3, x4, y4)):
+        held.append((x_got, ((0, c, k, 1, "c_mine"), (c, e, k - 1, 1, "e_mine"), (c + e, e, k - 1, 1, "e_other"))))
+        held.append((y_got, ((0, c, k - 1, 0, "c_other"), (c, c, k - 1, 1, "c_other"), (2 * c, e, k, 0, "e_other"))))
+    held.append((x5, ((0, e, 3, 1, "e_mine"), (e, e, 3, 1, "e_other"))))
+    held.append((y5, ((0, c, 3, 0, "c_other"), (c, c, 3, 1, "c_other"))))
+    pieces, plan = [], Plan([], rows, PARTS)
+    for value, parts in held:
+        for other_core, piece in ((0, value), (1, send("core", value))):
             for start, count, steps, other_x, part in parts:
-                spans.append((len(pieces), start, count, (steps, other_x, other_core, part)))
+                plan.spans.append((len(pieces), start, count, (steps, other_x, other_core, part)))
             pieces.append(piece)
-
-    both(shard, (0, rows, 0, 0, "all"))
-    both(x0c, (0, c, 0, 1, "c_mine"))
-    both(x0e, (0, size_e, 0, 1, "e"))
-    both(y0, (0, c, 0, 1, "c_other"))
-    rounds = ((zc1, ze1, xc1, ye1, yc1, xe1), (zc2, ze2, xc2, ye2, yc2, xe2), (zc3, ze3, xc3, ye3, yc3, xe3))
-    for k, (zc, ze, xc, ye, yc, xe) in enumerate(rounds, 1):
-        both(zc, (0, c, k, 0, "c_mine"))
-        both(ze, (0, e, k, 0, "e_mine"))
-        both(xc, (0, c, k, 1, "c_mine"))
-        both(ye, (0, size_e - e, k, 0, "e_other"))
-        both(yc, (0, c, k, 0, "c_other"), (c, c, k, 1, "c_other"))
-        both(xe, (0, e, k, 1, "e_mine"), (e, size_e - e, k, 1, "e_other"))
-    return pieces, plan
+    return pieces, plan, small
 
 
 def add_low(a, b):
     return (a.astype(f32) + b.astype(f32)).astype(bf16)
 
 
-def scatter_sum(grads, rows, first):
-    c, e = first, rows // 2 - first
-    z, x, core, rep = position()
-    stacked = grads.reshape(4, 2, 2, rows, D)
+def scatter_sum(grads, small, sums, half):
+    rows = grads[0].shape[0] // 2
+    c, e = half, rows // 2 - half
+    rep = lax.axis_index("dp")
     cut = lax.dynamic_slice_in_dim
-    ring_c = ring_e = None
-    last = {"x": [], "y": [], "z": []}
-
-    def link(name, swap, value):
-        done = last[name]
-        got = swap(value, *done[-2:-1])
-        done.append(got)
-        return got
-
+    links = {"x": [], "y": [], "z": []}
+
+    def link(name, *values):
+        done = links[name]
+        first = hold(values[0], *done[-2:-1])
+        done.append(send(name, first, *values[1:]))
+        return done[-1]
+
+    def packed():
+        high = sums.astype(bf16)
+        low = (sums - high.astype(f32)).astype(bf16)
+        return jnp.concatenate([small, jnp.stack([high, low] + [jnp.zeros_like(high)] * 6)])
+
+    def added(others):
+        total, total_sums = small.astype(f32), sums
+        for other in others:
+            total = total + other[:16].astype(f32)
+            total_sums = total_sums + (other[16].astype(f32) + other[17].astype(f32))
+        return total.astype(bf16), total_sums
+
+    small, sums = added([send("core", packed())])
+    rider, riders = packed(), []
+    ring_c = ring_e = to_y = None
     for k in (1, 2, 3, 0):
-        target = lax.rem(z - k + 4, 4)
-
-        def pick(at_x, at_core):
-            return lax.dynamic_slice(stacked, (target, at_x, at_core, 0, 0), (1, 1, 1, rows, D)).reshape(rows, D)
-
-        got = swap_core(jnp.concatenate([pick(x, 1 - core), pick(1 - x, 1 - core)]))
-        own, other = add_low(got[:rows], pick(x, core)), add_low(got[rows:], pick(1 - x, core))
-        yc = link("y", swap_y, jnp.concatenate([cut(own, (1 - rep) * c, c), cut(other, (1 - rep) * c, c)]))
-        xe = link("x", swap_x, other[2 * c :])
-        own_c, other_c = add_low(cut(own, rep * c, c), yc[:c]), add_low(cut(other, rep * c, c), yc[c:])
-        own_e = add_low(own[2 * c :], xe)
-        xc = link("x", swap_x, other_c)
-        ye = link("y", swap_y, cut(own_e, (1 - rep) * e, e))
-        sum_c = own_c.astype(f32) + xc.astype(f32)
+        keep, got = grads[k], send("core", grads[4 + k])
+        part = lambda first, count: add_low(keep[first : first + count], got[first : first + count])
+        to_y = part(2 * c, 2 * c)
+        yc = link("y", to_y)
+        xe = link("x", part(4 * c, 2 * e))
+        both_c = add_low(part(0, 2 * c), yc)
+        own_e = add_low(part(4 * c + 2 * e, 2 * e), xe)
+        if k == 0:
+            small, sums = added(riders)
+            xc = link("x", both_c[c:], packed())
+            small, sums = added([xc[c:]])
+        else:
+            xc = link("x", both_c[c:])
+        ye = link("y", cut(own_e, (1 - rep) * e, e))
+        sum_c = both_c[:c].astype(f32) + xc[:c].astype(f32)
         sum_e = cut(own_e, rep * e, e).astype(f32) + ye.astype(f32)
         if ring_c is not None:
-            sum_c, sum_e = sum_c + ring_c.astype(f32), sum_e + ring_e.astype(f32)
+            sum_c, sum_e = sum_c + ring_c.astype(f32), sum_e + ring_e[:e].astype(f32)
         sum_c, sum_e = sum_c.astype(bf16), sum_e.astype(bf16)
         if k:
-            ring_c, ring_e = link("z", next_z, sum_c), link("z", next_z, sum_e)
-    back = swap_y(jnp.concatenate([sum_c, sum_e]))
+            ring_c, ring_e = link("z", sum_c), link("z", sum_e, rider)
+            rider = ring_e[e:]
+            riders.append(rider)
+    back = send("y", sum_c, sum_e, packed())
+    small, sums = added([back[c + e :]])
     order = lambda a, b: [jnp.where(rep == 0, a, b), jnp.where(rep == 0, b, a)]
-    return jnp.concatenate(order(sum_c, back[:c]) + order(sum_e, back[c:]))
+    return jnp.concatenate(order(sum_c, back[:c]) + order(sum_e, back[c : c + e])), small, sums
 
 
 def row_rates(row_index):
@@ -529,17 +563,18 @@
     if paths:
         placed = lax.dynamic_update_slice(jnp.zeros((16, D), bf16), vec_low, (0, lanes * index))
         placed = jnp.where(lax.axis_index("dp") == 0, placed, jnp.zeros_like(placed))
-        small = sum_small(jnp.concatenate([placed, jnp.full((8, D), active).astype(bf16)]))
+        layout = Layout(shard_rows, HALF)
+        pieces, plan, small = gather(mat_low, jnp.concatenate([placed, jnp.full((8, D), active).astype(bf16)]))
         vectors, active_count = small[:16].astype(f32), small[16, 0].astype(f32)
-        pieces, plan = gather_pieces(mat_low, paths[0])
     else:
         pieces = [lax.all_gather(mat_low, "fsdp", axis=0, tiled=True)]
-        plan = Plan([(0, 0, MROWS, 0)], 3 * D)
+        plan, layout = Plan([(0, 0, MROWS, 0)], 3 * D), Layout(shard_rows, 0)
         vectors = lax.all_gather(vec_low, "fsdp", axis=1, tiled=True).astype(f32)
         active_count = lax.psum(active, ("dp", "fsdp"))
     qkv, context, stats = attn_fwd(plan, pieces, place, lengths, tokens, vectors)
-    block_out, grad_attn, grad_ctx, vec_grad, sums, mat_grad = ffn(
+    block_out, grad_attn, grad_ctx, vec_grad, sums, *mat_grad = ffn(
         plan,
+        layout,
         pieces,
         place,
         labels,
@@ -550,10 +585,10 @@
         context.reshape(toks, D),
         out_grad.reshape(toks, D),
         vectors,
-        MROWS,
-    )
-    input_grad, head_grad, mat_grad = attn_bwd(
+    )
+    input_grad, head_grad, *mat_grad = attn_bwd(
         plan,
+        layout,
         pieces,
         place,
         lengths,
@@ -568,12 +603,11 @@
     vec_grad = jnp.concatenate([head_grad[:2], vec_grad[2:]])
     sums = jnp.sum(sums, axis=0)
     if paths:
-        mat_total = scatter_sum(mat_grad, shard_rows, paths[1]).astype(f32)
-        small = sum_small(jnp.concatenate([vec_grad, jnp.pad(sums[None], ((0, 7), (0, D - 128)))]))
-        vec_total = lax.dynamic_slice(small, (0, lanes * index), (16, lanes))
-        sums = small[16, :4]
+        mat_total, vec_total, sums = scatter_sum(mat_grad, vec_grad.astype(bf16), jnp.pad(sums, (0, D - 128)), HALF)
+        mat_total = mat_total.astype(f32)
+        vec_total = lax.dynamic_slice(vec_total, (0, lanes * index), (16, lanes)).astype(f32)
     else:
-        part = lax.psum_scatter(mat_grad, "fsdp", scatter_dimension=0, tiled=True)
+        part = lax.psum_scatter(mat_grad[0], "fsdp", scatter_dimension=0, tiled=True)
         mat_total = lax.psum(part, "dp").astype(f32)
         part = lax.psum_scatter(vec_grad.astype(bf16), "fsdp", scatter_dimension=1, tiled=True)
         vec_total = lax.psum(part, "dp").astype(f32)
@@ -612,7 +646,7 @@
     rows = P(("dp", "fsdp"), None, None)
     each = P(("dp", "fsdp"))
     mat, vec = P("fsdp", None), P(None, "fsdp")
-    paths = (160, 160) if (mesh.shape["dp"], mesh.shape["fsdp"]) == (2, FSDP) else None
+    paths = (mesh.shape["dp"], mesh.shape["fsdp"]) == (2, FSDP)
     return jax.shard_map(
         functools.partial(on_device, paths),
         mesh=mesh,

time: 355 us -> 339 us (0.955)
  starting transfers between devices: 67 us -> 42.2 us
  waiting for transfers between devices: 124 us -> 111 us
  other arithmetic: 26.7 us -> 36.9 us
  Pallas kernels: 120 us -> 130 us
    ppermute x80 -> x60, starting transfers between devices: 67 us -> 42.2 us  [send(): lax.ppermute(values[0] if len(values) == 1 else jnp.concatenate(values),...]
    convert_element_type x9 -> x16, other arithmetic: 7.3 us -> 21.4 us  [add_low(): return (a.astype(f32) + b.astype(f32)).astype(bf16)]
    ppermute x80 -> x60, waiting for transfers between devices: 124 us -> 111 us  [send(): lax.ppermute(values[0] if len(values) == 1 else jnp.concatenate(values),...]
    pallas_call x2, Pallas kernels: 103 us -> 113 us  [the longest x1 65.2 us: ffn(): pl.pallas_call(functools.partial(ffn_kernel, plan, layout, n, tiles, low)...]
    concatenate x16 -> x13, other arithmetic: 5.94 us -> 0.53 us  [send(): jnp.concatenate(values)]
    reshape x1 -> x0, local copies, waits for them, and re-layouts: 3.71 us -> none  [pick(): lax.dynamic_slice(stacked, (target, at_x, at_core, 0, 0), (1, 1, 1, rows,...]
  transfers between devices with their start and end apart: 80 -> 60, of which waited for: 36 -> 26; matrix products, arithmetic and copies ran while one was open for 6% -> 10% of each run, Pallas kernels for 0% -> 0%
where the time goes in v2:
time: 339 us; the launch traced here: 335 us
  Pallas kernels  130 us (38%)
  waiting for transfers between devices  111 us (33%)
  starting transfers between devices  42.2 us (12%)
  other arithmetic  36.9 us (11%)
  local copies, waits for them, and re-layouts  10.9 us (3%)
  between operations  4.63 us (1%)
    ppermute x60, waiting for transfers between devices, send(): lax.ppermute(values[0] if len(values) == 1 else jnp.concatenate(values),...  111 us
    pallas_call x1, Pallas kernels, ffn(): pl.pallas_call(functools.partial(ffn_kernel, plan, layout, n, tiles, low)...  65.2 us
    pallas_call x1, Pallas kernels, attn_bwd(): pl.pallas_call(functools.partial(attn_bwd_kernel, plan, layout, n, S), gr...  47.5 us
    ppermute x60, starting transfers between devices, send(): lax.ppermute(values[0] if len(values) == 1 else jnp.concatenate(values),...  42.2 us
    convert_element_type x16, other arithmetic, add_low(): return (a.astype(f32) + b.astype(f32)).astype(bf16)  21.4 us
    pallas_call x1, Pallas kernels, attn_fwd(): pl.pallas_call(functools.partial(attn_fwd_kernel, plan, n), grid=(S,), na...  17.2 us
  transfers between devices with their start and end apart: 60, of which 26 were waited for; matrix products, arithmetic and copies ran while one was open for 10% of the time, Pallas kernels for 0%

profile of v2, /device:TPU:0, one launch (start us, length us, event | category | flops | bytes accessed | tf_op | source)
XLA Modules:
  0.0 335.2 jit_solution(9653341711658430704)
XLA Ops:
  2.4 3.0 collective-permute-start.10
  8.8 12.2 %collective-permute-done.refs_2_ = bf16[296,768]{1,0:T(8,128)(2,1)S(1)} collective-permute-done((bf16[296,768]{1,0:T(8,128)(2,1)S(1)}, bf16[296,768]{1,0:T(8,128)(2,1)S(1)}, u32[]{:S(2)}, u32[]{:S(2)}) %collective-permute-start) | collective-permute-done | bytes 454688 | tf_op jit(solution)/shard_map/ppermute | solution.py:401
  23.6 10.4 %collective-permute-done.1.refs_6_ = bf16[296,768]{1,0:T(8,128)(2,1)S(1)} collective-permute-done((bf16[296,768]{1,0:T(8,128)(2,1)S(1)}, bf16[296,768]{1,0:T(8,128)(2,1)S(1)}, u32[]{:S(2)}, u32[]{:S(2)}) %collective-permute-start.1) | collective-permute-done | bytes 454688 | tf_op jit(solution)/shard_map/ppermute | solution.py:401
  37.3 9.8 %collective-permute-done.3.refs_10_ = bf16[296,768]{1,0:T(8,128)(2,1)S(1)} collective-permute-done((bf16[296,768]{1,0:T(8,128)(2,1)S(1)}, bf16[296,768]{1,0:T(8,128)(2,1)S(1)}, u32[]{:S(2)}, u32[]{:S(2)}) %collective-permute-start.3) | collective-permute-done | bytes 454688 | tf_op jit(solution)/shard_map/ppermute | solution.py:401
  51.9 3.2 collective-permute-done.11.refs_4_
  55.7 7.4 %collective-permute-done.16.refs_8_ = bf16[160,768]{1,0:T(8,128)(2,1)S(1)} collective-permute-done((bf16[160,768]{1,0:T(8,128)(2,1)S(1)}, bf16[160,768]{1,0:T(8,128)(2,1)S(1)}, u32[]{:S(2)}, u32[]{:S(2)}) %collective-permute-start.16) | collective-permute-done | bytes 245792 | tf_op jit(solution)/shard_map/ppermute | solution.py:401
  67.6 6.8 %collective-permute-done.20.refs_12_ = bf16[160,768]{1,0:T(8,128)(2,1)S(1)} collective-permute-done((bf16[160,768]{1,0:T(8,128)(2,1)S(1)}, bf16[160,768]{1,0:T(8,128)(2,1)S(1)}, u32[]{:S(2)}, u32[]{:S(2)}) %collective-permute-start.20) | collective-permute-done | bytes 245792 | tf_op jit(solution)/shard_map/ppermute | solution.py:401
  78.1 7.6 %collective-permute-done.21.refs_28_ = bf16[288,768]{1,0:T(8,128)(2,1)} collective-permute-done((bf16[288,768]{1,0:T(8,128)(2,1)S(1)}, bf16[288,768]{1,0:T(8,128)(2,1)}, u32[]{:S(2)}, u32[]{:S(2)}) %collective-permute-start.21) | collective-permute-done | bytes 442400 | tf_op jit(solution)/shard_map/ppermute | solution.py:401
  92.7 17.2 %attn_fwd.1 = (bf16[2,512,2304]{2,1,0:T(8,128)(2,1)}, bf16[2,512,768]{2,1,0:T(8,128)(2,1)}, f32[2,128,512]{2,1,0:T(8,128)}) custom-call(s32[4]{0:T(128)S(1)} %pad_add_fusion.1.place, s32[2]{0:T(128)S(1)} %copy-done.16, bf16[2,512,768]{2,1,0:T(8,128)(2,1)} %x_ref.3, f32[16,768]{1,0:T(8,128)S(1)} %slice_convert_fusion.1.vec_ref, bf16[624,768]{1,0:T(8,128)(2,1)} %copy-done.18, ...), custom_call_target="tpu_custom_call" | custom-call | flops 8000000000 | bytes 14000000 | tf_op jit(solution)/shard_map/attn_fwd/pallas_call | solution.py:175
  110.0 65.2 %ffn.1 = (bf16[1024,768]{1,0:T(8,128)(2,1)}, f32[1024,768]{1,0:T(8,128)}, bf16[1024,768]{1,0:T(8,128)(2,1)}, f32[16,768]{1,0:T(8,128)}, f32[16,128]{1,0:T(8,128)...) custom-call(s32[4]{0:T(128)} %copy-done.4, ...), custom_call_target="tpu_custom_call" | custom-call | flops 32999999488 | bytes 40000000 | tf_op jit(solution)/shard_map/ffn/pallas_call | solution.py:303
  175.3 47.5 %attn_bwd.1 = (bf16[2,512,768]{2,1,0:T(8,128)(2,1)}, f32[8,768]{1,0:T(8,128)}, bf16[1248,768]{1,0:T(8,128)(2,1)}, bf16[1248,768]{1,0:T(8,128)(2,1)}, bf16[1248,7...) custom-call(s32[4]{0:T(128)} %copy-done.4, ...), custom_call_target="tpu_custom_call", output_to_operand_aliasing={{2}: (40, {}), {3}: (41, {}), {4}: (42, {}), {5}: (43, {}),... | custom-call | flops 16000000000 | bytes 24000000 | tf_op jit(solution)/shard_map/attn_bwd/pallas_call | solution.py:371
  232.6 1.9 add_convert_fusion.8
  237.4 2.5 add_convert_fusion.16
  239.9 1.9 add_convert_fusion.19
  252.0 3.8 %collective-permute-done.50 = bf16[160,768]{1,0:T(8,128)(2,1)} collective-permute-done((bf16[160,768]{1,0:T(8,128)(2,1)}, bf16[160,768]{1,0:T(8,128)(2,1)}, u32[]{:S(2)}, u32[]{:S(2)}) %collective-permute-start.50) | collective-permute-done | bytes 245792 | tf_op jit(solution)/shard_map/ppermute | solution.py:401
  257.6 7.1 %collective-permute-done.38 = bf16[304,768]{1,0:T(8,128)(2,1)} collective-permute-done((bf16[304,768]{1,0:T(8,128)(2,1)}, bf16[304,768]{1,0:T(8,128)(2,1)}, u32[]{:S(2)}, u32[]{:S(2)}) %collective-permute-start.38) | collective-permute-done | bytes 466976 | tf_op jit(solution)/shard_map/ppermute | solution.py:401
  272.0 3.9 %collective-permute-done.39 = bf16[152,768]{1,0:T(8,128)(2,1)S(1)} collective-permute-done((bf16[152,768]{1,0:T(8,128)(2,1)S(1)}, bf16[152,768]{1,0:T(8,128)(2,1)S(1)}, u32[]{:S(2)}, u32[]{:S(2)}) %collective-permute-start.39) | collective-permute-done | bytes 233504 | tf_op jit(solution)/shard_map/ppermute | solution.py:401
  276.8 5.0 %collective-permute-done.51 = bf16[160,768]{1,0:T(8,128)(2,1)S(1)} collective-permute-done((bf16[160,768]{1,0:T(8,128)(2,1)S(1)}, bf16[160,768]{1,0:T(8,128)(2,1)S(1)}, u32[]{:S(2)}, u32[]{:S(2)}) %collective-permute-start.51) | collective-permute-done | bytes 245792 | tf_op jit(solution)/shard_map/ppermute | solution.py:401
  290.2 2.9 collective-permute-done.43
  293.3 4.5 %collective-permute-done.57 = bf16[304,768]{1,0:T(8,128)(2,1)S(1)} collective-permute-done((bf16[304,768]{1,0:T(8,128)(2,1)S(1)}, bf16[304,768]{1,0:T(8,128)(2,1)S(1)}, u32[]{:S(2)}, u32[]{:S(2)}) %collective-permute-start.57) | collective-permute-done | bytes 466976 | tf_op jit(solution)/shard_map/ppermute | solution.py:401
  307.5 4.3 %collective-permute-done.53 = bf16[184,768]{1,0:T(8,128)(2,1)S(1)} collective-permute-done((bf16[184,768]{1,0:T(8,128)(2,1)S(1)}, bf16[184,768]{1,0:T(8,128)(2,1)S(1)}, u32[]{:S(2)}, u32[]{:S(2)}) %collective-permute-start.53) | collective-permute-done | bytes 282656 | tf_op jit(solution)/shard_map/ppermute | solution.py:401
  311.9 3.5 %collective-permute-done.56 = bf16[160,768]{1,0:T(8,128)(2,1)S(1)} collective-permute-done((bf16[160,768]{1,0:T(8,128)(2,1)S(1)}, bf16[160,768]{1,0:T(8,128)(2,1)S(1)}, u32[]{:S(2)}, u32[]{:S(2)}) %collective-permute-start.56) | collective-permute-done | bytes 245792 | tf_op jit(solution)/shard_map/ppermute | solution.py:401
  316.4 8.5 %collective-permute-done.59 = bf16[336,768]{1,0:T(8,128)(2,1)S(1)} collective-permute-done((bf16[336,768]{1,0:T(8,128)(2,1)S(1)}, bf16[336,768]{1,0:T(8,128)(2,1)S(1)}, u32[]{:S(2)}, u32[]{:S(2)}) %collective-permute-start.59) | collective-permute-done | bytes 516128 | tf_op jit(solution)/shard_map/ppermute | solution.py:401
  327.7 6.2 %fusion.28 = (bf16[624,768]{1,0:T(8,128)(2,1)}, f32[624,768]{1,0:T(8,128)}, f32[624,768]{1,0:T(8,128)}, f32[624,768]{1,0:T(8,128)}) fusion(f32[624,768]{1,0:T(8,128)S(1)} %copy-done.17, f32[624]{0:T(1024)S(1)} %select_select_fusion, bf16[152,768]{1,0:T(8,128)(2,1)S(1)} %get-tuple-element.132, bf16[152,768]{1,0:T(8,128)(2,1)S(1)} %get-tuple-element.131, ...), kind=kLoop, calls=%fused_computation.127 | loop fusion | flops 11501568 | bytes 13420992 | tf_op jit(solution)/shard_map/convert_element_type | solution.py:634
  (320 shorter events, 84.4 us)
Async XLA Ops:
  2.4 18.7 %collective-permute-start.10 = (bf16[336,768]{1,0:T(8,128)(2,1)S(1)}, bf16[336,768]{1,0:T(8,128)(2,1)S(1)}, u32[]{:S(2)}, u32[]{:S(2)}) collective-permute-start(bf16[336,768]{1,0:T(8,128)(2,1)S(1)} %pad_maximum_fusion.5), channel_id=1, source_target_pairs={{0,2},{1,3},{2,0},{3,1},{4,6},{5,7},{6,4},{7,5},{8,10},{9,11},{10,... | collective-permute-start | bytes 1548296 | tf_op jit(solution)/shard_map/ppermute | solution.py:401
  7.1 13.9 %collective-permute-start = (bf16[296,768]{1,0:T(8,128)(2,1)S(1)}, bf16[296,768]{1,0:T(8,128)(2,1)S(1)}, u32[]{:S(2)}, u32[]{:S(2)}) collective-permute-start(bf16[296,768]{1,0:T(8,128)(2,1)S(1)} %maximum_maximum_fusion), channel_id=1, source_target_pairs={{0,4},{1,5},{2,6},{3,7},{4,8},{5,9},{6,10},{7,11},{8,12},{9,13},{1... | collective-permute-start | bytes 1363976 | tf_op jit(solution)/shard_map/ppermute | solution.py:401
  21.0 13.0 %collective-permute-start.1 = (bf16[296,768]{1,0:T(8,128)(2,1)S(1)}, bf16[296,768]{1,0:T(8,128)(2,1)S(1)}, u32[]{:S(2)}, u32[]{:S(2)}) collective-permute-start(bf16[296,768]{1,0:T(8,128)(2,1)S(1)} %collective-permute-done.refs_2_), channel_id=1, source_target_pairs={{0,4},{1,5},{2,6},{3,7},{4,8},{5,9},{6,10},{7,11},{8,12},{9,13},{1... | collective-permute-start | bytes 1363976 | tf_op jit(solution)/shard_map/ppermute | solution.py:401
  21.1 12.9 %collective-permute-start.12 = (bf16[272,768]{1,0:T(8,128)(2,1)S(1)}, bf16[272,768]{1,0:T(8,128)(2,1)S(1)}, u32[]{:S(2)}, u32[]{:S(2)}) collective-permute-start(bf16[272,768]{1,0:T(8,128)(2,1)S(1)} %pad_maximum_fusion.9), channel_id=1, source_target_pairs={{0,16},{16,0},{1,17},{17,1},{2,18},{18,2},{3,19},{19,3},{4,20},{20... | collective-permute-start | bytes 1253384 | tf_op jit(solution)/shard_map/ppermute | solution.py:401
  34.1 14.2 %collective-permute-start.13 = (bf16[416,768]{1,0:T(8,128)(2,1)S(1)}, bf16[416,768]{1,0:T(8,128)(2,1)S(1)}, u32[]{:S(2)}, u32[]{:S(2)}) collective-permute-start(bf16[416,768]{1,0:T(8,128)(2,1)S(1)} %pad_maximum_fusion.2), channel_id=1, source_target_pairs={{0,2},{1,3},{2,0},{3,1},{4,6},{5,7},{6,4},{7,5},{8,10},{9,11},{10,... | collective-permute-start | bytes 1916936 | tf_op jit(solution)/shard_map/ppermute | solution.py:401
  35.4 15.3 %collective-permute-start.4 = (bf16[400,768]{1,0:T(8,128)(2,1)S(1)}, bf16[400,768]{1,0:T(8,128)(2,1)S(1)}, u32[]{:S(2)}, u32[]{:S(2)}) collective-permute-start(bf16[400,768]{1,0:T(8,128)(2,1)S(1)} %pad_maximum_fusion.3), channel_id=1, source_target_pairs={{0,16},{16,0},{1,17},{17,1},{2,18},{18,2},{3,19},{19,3},{4,20},{20... | collective-permute-start | bytes 1843208 | tf_op jit(solution)/shard_map/ppermute | solution.py:401
  36.7 18.4 %collective-permute-start.8 = (bf16[624,768]{1,0:T(8,128)(2,1)S(1)}, bf16[624,768]{1,0:T(8,128)(2,1)S(1)}, u32[]{:S(2)}, u32[]{:S(2)}) collective-permute-start(bf16[624,768]{1,0:T(8,128)(2,1)S(1)} %convert_element_type.472.refs_0_), channel_id=1, source_target_pairs={{0,1},{1,0},{2,3},{3,2},{4,5},{5,4},{6,7},{7,6},{8,9},{9,8},{10,11... | collective-permute-start | bytes 2875400 | tf_op jit(solution)/shard_map/ppermute | solution.py:401
  36.7 18.3 %collective-permute-start.9 = (bf16[296,768]{1,0:T(8,128)(2,1)S(1)}, bf16[296,768]{1,0:T(8,128)(2,1)}, u32[]{:S(2)}, u32[]{:S(2)}) collective-permute-start(bf16[296,768]{1,0:T(8,128)(2,1)S(1)} %collective-permute-done.refs_2_), channel_id=1, source_target_pairs={{0,1},{1,0},{2,3},{3,2},{4,5},{5,4},{6,7},{7,6},{8,9},{9,8},{10,11... | collective-permute-start | bytes 1363976 | tf_op jit(solution)/shard_map/ppermute | solution.py:401
  48.4 14.6 %collective-permute-start.17 = (bf16[400,768]{1,0:T(8,128)(2,1)S(1)}, bf16[400,768]{1,0:T(8,128)(2,1)}, u32[]{:S(2)}, u32[]{:S(2)}) collective-permute-start(bf16[400,768]{1,0:T(8,128)(2,1)S(1)} %pad_maximum_fusion.4), channel_id=1, source_target_pairs={{0,16},{16,0},{1,17},{17,1},{2,18},{18,2},{3,19},{19,3},{4,20},{20... | collective-permute-start | bytes 1843208 | tf_op jit(solution)/shard_map/ppermute | solution.py:401
  50.8 14.4 %collective-permute-start.5 = (bf16[440,768]{1,0:T(8,128)(2,1)S(1)}, bf16[440,768]{1,0:T(8,128)(2,1)}, u32[]{:S(2)}, u32[]{:S(2)}) collective-permute-start(bf16[440,768]{1,0:T(8,128)(2,1)S(1)} %pad_maximum_fusion.1), channel_id=1, source_target_pairs={{0,2},{1,3},{2,0},{3,1},{4,6},{5,7},{6,4},{7,5},{8,10},{9,11},{10,... | collective-permute-start | bytes 2027528 | tf_op jit(solution)/shard_map/ppermute | solution.py:401
  77.5 13.0 %collective-permute-start.28 = (bf16[440,768]{1,0:T(8,128)(2,1)}, bf16[440,768]{1,0:T(8,128)(2,1)}, u32[]{:S(2)}, u32[]{:S(2)}) collective-permute-start(bf16[440,768]{1,0:T(8,128)(2,1)} %collective-permute-done.5.refs_24_), channel_id=1, source_target_pairs={{0,1},{1,0},{2,3},{3,2},{4,5},{5,4},{6,7},{7,6},{8,9},{9,8},{10,11... | collective-permute-start | bytes 2027528 | tf_op jit(solution)/shard_map/ppermute | solution.py:401
  223.5 13.0 %collective-permute-start.45 = (bf16[1248,768]{1,0:T(8,128)(2,1)}, bf16[1248,768]{1,0:T(8,128)(2,1)S(1)}, u32[]{:S(2)}, u32[]{:S(2)}) collective-permute-start(bf16[1248,768]{1,0:T(8,128)(2,1)} %get-tuple-element.99), channel_id=1, source_target_pairs={{0,1},{1,0},{2,3},{3,2},{4,5},{5,4},{6,7},{7,6},{8,9},{9,8},{10,11... | collective-permute-start | bytes 5750792 | tf_op jit(solution)/shard_map/ppermute | solution.py:401
  228.5 13.3 %collective-permute-start.34 = (bf16[304,768]{1,0:T(8,128)(2,1)S(1)}, bf16[304,768]{1,0:T(8,128)(2,1)S(1)}, u32[]{:S(2)}, u32[]{:S(2)}) collective-permute-start(bf16[304,768]{1,0:T(8,128)(2,1)S(1)} %add_convert_fusion.22), channel_id=1, source_target_pairs={{0,2},{1,3},{2,0},{3,1},{4,6},{5,7},{6,4},{7,5},{8,10},{9,11},{10,... | collective-permute-start | bytes 1400840 | tf_op jit(solution)/shard_map/ppermute | solution.py:401
  231.0 13.7 %collective-permute-start.46 = (bf16[320,768]{1,0:T(8,128)(2,1)S(1)}, bf16[320,768]{1,0:T(8,128)(2,1)S(1)}, u32[]{:S(2)}, u32[]{:S(2)}) collective-permute-start(bf16[320,768]{1,0:T(8,128)(2,1)S(1)} %add_convert_fusion.7), channel_id=1, source_target_pairs={{0,16},{16,0},{1,17},{17,1},{2,18},{18,2},{3,19},{19,3},{4,20},{20... | collective-permute-start | bytes 1474568 | tf_op jit(solution)/shard_map/ppermute | solution.py:401
  248.5 16.2 %collective-permute-start.38 = (bf16[304,768]{1,0:T(8,128)(2,1)}, bf16[304,768]{1,0:T(8,128)(2,1)}, u32[]{:S(2)}, u32[]{:S(2)}) collective-permute-start(bf16[304,768]{1,0:T(8,128)(2,1)} %add_convert_fusion.19), channel_id=1, source_target_pairs={{0,2},{1,3},{2,0},{3,1},{4,6},{5,7},{6,4},{7,5},{8,10},{9,11},{10,... | collective-permute-start | bytes 1400840 | tf_op jit(solution)/shard_map/ppermute | solution.py:401
  249.5 18.4 %collective-permute-start.47 = (bf16[320,768]{1,0:T(8,128)(2,1)}, bf16[320,768]{1,0:T(8,128)(2,1)}, u32[]{:S(2)}, u32[]{:S(2)}) collective-permute-start(bf16[320,768]{1,0:T(8,128)(2,1)} %add_convert_fusion.8), channel_id=1, source_target_pairs={{0,16},{16,0},{1,17},{17,1},{2,18},{18,2},{3,19},{19,3},{4,20},{20... | collective-permute-start | bytes 1474568 | tf_op jit(solution)/shard_map/ppermute | solution.py:401
  251.2 16.7 %collective-permute-start.36 = (bf16[176,768]{1,0:T(8,128)(2,1)S(1)}, bf16[176,768]{1,0:T(8,128)(2,1)S(1)}, u32[]{:S(2)}, u32[]{:S(2)}) collective-permute-start(bf16[176,768]{1,0:T(8,128)(2,1)S(1)} %concatenate.77), channel_id=1, source_target_pairs={{0,4},{1,5},{2,6},{3,7},{4,8},{5,9},{6,10},{7,11},{8,12},{9,13},{1... | collective-permute-start | bytes 811016 | tf_op jit(solution)/shard_map/ppermute | solution.py:401
  256.8 20.1 %collective-permute-start.54 = (bf16[160,768]{1,0:T(8,128)(2,1)S(1)}, bf16[160,768]{1,0:T(8,128)(2,1)S(1)}, u32[]{:S(2)}, u32[]{:S(2)}) collective-permute-start(bf16[160,768]{1,0:T(8,128)(2,1)S(1)} %add_convert_fusion.27), channel_id=1, source_target_pairs={{0,4},{1,5},{2,6},{3,7},{4,8},{5,9},{6,10},{7,11},{8,12},{9,13},{1... | collective-permute-start | bytes 737288 | tf_op jit(solution)/shard_map/ppermute | solution.py:401
  264.7 18.6 %collective-permute-start.42 = (bf16[304,768]{1,0:T(8,128)(2,1)}, bf16[304,768]{1,0:T(8,128)(2,1)S(1)}, u32[]{:S(2)}, u32[]{:S(2)}) collective-permute-start(bf16[304,768]{1,0:T(8,128)(2,1)} %add_convert_fusion.16), channel_id=1, source_target_pairs={{0,2},{1,3},{2,0},{3,1},{4,6},{5,7},{6,4},{7,5},{8,10},{9,11},{10,... | collective-permute-start | bytes 1400840 | tf_op jit(solution)/shard_map/ppermute | solution.py:401
  270.5 15.7 %collective-permute-start.48 = (bf16[320,768]{1,0:T(8,128)(2,1)S(1)}, bf16[320,768]{1,0:T(8,128)(2,1)S(1)}, u32[]{:S(2)}, u32[]{:S(2)}) collective-permute-start(bf16[320,768]{1,0:T(8,128)(2,1)S(1)} %add_convert_fusion.9), channel_id=1, source_target_pairs={{0,16},{16,0},{1,17},{17,1},{2,18},{18,2},{3,19},{19,3},{4,20},{20... | collective-permute-start | bytes 1474568 | tf_op jit(solution)/shard_map/ppermute | solution.py:401
  282.6 23.6 %collective-permute-start.55 = (bf16[160,768]{1,0:T(8,128)(2,1)}, bf16[160,768]{1,0:T(8,128)(2,1)}, u32[]{:S(2)}, u32[]{:S(2)}) collective-permute-start(bf16[160,768]{1,0:T(8,128)(2,1)} %add_convert_fusion.26), channel_id=1, source_target_pairs={{0,4},{1,5},{2,6},{3,7},{4,8},{5,9},{6,10},{7,11},{8,12},{9,13},{1... | collective-permute-start | bytes 737288 | tf_op jit(solution)/shard_map/ppermute | solution.py:401
  284.9 12.9 %collective-permute-start.57 = (bf16[304,768]{1,0:T(8,128)(2,1)S(1)}, bf16[304,768]{1,0:T(8,128)(2,1)S(1)}, u32[]{:S(2)}, u32[]{:S(2)}) collective-permute-start(bf16[304,768]{1,0:T(8,128)(2,1)S(1)} %copy-done.27), channel_id=1, source_target_pairs={{0,2},{1,3},{2,0},{3,1},{4,6},{5,7},{6,4},{7,5},{8,10},{9,11},{10,... | collective-permute-start | bytes 1400840 | tf_op jit(solution)/shard_map/ppermute | solution.py:401
  287.5 17.4 %collective-permute-start.52 = (bf16[160,768]{1,0:T(8,128)(2,1)S(1)}, bf16[160,768]{1,0:T(8,128)(2,1)}, u32[]{:S(2)}, u32[]{:S(2)}) collective-permute-start(bf16[160,768]{1,0:T(8,128)(2,1)S(1)} %slice.457), channel_id=1, source_target_pairs={{0,2},{1,3},{2,0},{3,1},{4,6},{5,7},{6,4},{7,5},{8,10},{9,11},{10,... | collective-permute-start | bytes 737288 | tf_op jit(solution)/shard_map/ppermute | solution.py:401
  288.4 15.2 %collective-permute-start.49 = (bf16[320,768]{1,0:T(8,128)(2,1)}, bf16[320,768]{1,0:T(8,128)(2,1)S(1)}, u32[]{:S(2)}, u32[]{:S(2)}) collective-permute-start(bf16[320,768]{1,0:T(8,128)(2,1)} %add_convert_fusion.10), channel_id=1, source_target_pairs={{0,16},{16,0},{1,17},{17,1},{2,18},{18,2},{3,19},{19,3},{4,20},{20... | collective-permute-start | bytes 1474568 | tf_op jit(solution)/shard_map/ppermute | solution.py:401
  (87 other events, 1411.6 us)
